TPU v7x, 128 devices: a whole 4x4x4 slice. The times are simulated.
128 devices in a mesh: wide: 16 (over y, z_lo, core), narrow: 8 (over x, z_hi).
Axes of the slice: x: 4, y: 4, z: 4 (z_hi: 2, z_lo: 2; z = z_hi * 2 + z_lo), core: 2. Of those that a mesh axis runs over, the one named last changes fastest.
Arguments:
- token_ids: int32 [4096], P('narrow'), may hold values from 0 to 50431
- group_ids: int32 [8], replicated, may hold values from 0 to 1
- prefix_lengths: int32 [2], replicated, may hold values from 1 to 512, as said below
- cached_lengths: int32 [8], replicated, may hold values from 0 to 2048, as said below
- embedding: bfloat16 [50432, 4096], P('narrow', 'wide'), may hold values from -6 to 6
- ln_gains: float32 [2, 4096], replicated, may hold values from 0.1 to 1.9
- qkv_weight: bfloat16 [4096, 12288], P('narrow', 'wide'), may hold values from -0.09375 to 0.09375
- out_weight: bfloat16 [4096, 4096], P('wide', 'narrow'), may hold values from -0.125 to 0.125
- up_weight: bfloat16 [4096, 16384], P('narrow', 'wide'), may hold values from -0.09375 to 0.09375
- down_weight: bfloat16 [16384, 4096], P('wide', 'narrow'), may hold values from -0.125 to 0.125
- prefix_keys: bfloat16 [2, 512, 4096], P(None, 'narrow', 'wide'), may hold values from -480 to 480
- prefix_values: bfloat16 [2, 512, 4096], P(None, 'narrow', 'wide'), may hold values from -6 to 6
- suffix_keys: bfloat16 [8, 2048, 4096], P('narrow', None, 'wide'), may hold values from -480 to 480
- suffix_values: bfloat16 [8, 2048, 4096], P('narrow', None, 'wide'), may hold values from -6 to 6
- final_gain: float32 [4096], replicated, may hold values from 0.1 to 1.9
- head_weight: bfloat16 [4096, 50432], P(None, ('wide', 'narrow')), may hold values from -0.25 to 0.25
Outputs:
- hidden_out: bfloat16 [4096, 4096], P('narrow', 'wide')
- last_rms: float32 [8], replicated
- max_logit: float32 [8], replicated
Inputs may be any that keep to these rules, and one draw needn't show every extreme that they name: `prefix_lengths`: every prefix holds at least one cached position, and some prefix holds exactly 512. `cached_lengths`: some request holds exactly 2048 cached private positions.
All inputs are finite; a program needn't handle non-finite values.
Results may differ from a plain program's by a relative error of at most 0.017.
Values may be sent and summed in bfloat16 or wider, within the bound.
A program may use at most 192 MiB of HBM per device.

v0:
```python
import math

import jax
import jax.numpy as jnp
from jax import lax
from jax.sharding import PartitionSpec as P

HD = 128
ROT = 32


NEG = -1e30


def layer_norm(rows, gain):
    values = rows.astype(jnp.float32)
    center = values - jnp.mean(values, axis=-1, keepdims=True)
    spread = jnp.mean(center * center, axis=-1, keepdims=True)
    return center * lax.rsqrt(spread + 1e-05) * gain


def rotate(values, places):
    half = ROT // 2
    freqs = jnp.power(10000.0, -(jnp.arange(half).astype(jnp.float32) * 2.0 / ROT))
    angles = places[:, None] * freqs[None, :]
    cosine = jnp.concatenate([jnp.cos(angles), jnp.cos(angles)], axis=-1)[:, None, :]
    sine = jnp.concatenate([jnp.sin(angles), jnp.sin(angles)], axis=-1)[:, None, :]
    turned = values[..., :ROT]
    swapped = jnp.concatenate([-turned[..., half:], turned[..., :half]], axis=-1)
    return jnp.concatenate([turned * cosine + swapped * sine, values[..., ROT:]], axis=-1)


def pick(table, index):
    match = index[:, None] == jnp.arange(table.shape[0], dtype=jnp.int32)[None, :]
    return jnp.sum(jnp.where(match, table[None, :], 0), axis=1)


def add_rows(left, piece):
    return jnp.dot(left, piece, preferred_element_type=jnp.float32)


def prefix_grid(query_grid, key_table, lengths, groups):
    group_count, span, width = key_table.shape
    heads = query_grid.shape[2]
    head_dim = query_grid.shape[3]
    place = jnp.arange(span, dtype=jnp.int32)
    group_range = jnp.arange(group_count, dtype=jnp.int32)
    valid = (place[None, None, :] < lengths[None, :, None]) & (
        groups[:, None, None] == group_range[None, :, None]
    )
    valid = valid.reshape(groups.shape[0], group_count * span)[:, None, None, :]
    scores = jnp.einsum(
        "rqhd,khd->rqhk",
        query_grid,
        key_table.reshape(group_count * span, heads, head_dim),
        preferred_element_type=jnp.float32,
    ) * (1.0 / math.sqrt(head_dim))
    return (jnp.where(valid, scores, NEG), valid)


def suffix_grid(query_grid, key_table, lengths):
    count, span, width = key_table.shape
    heads = query_grid.shape[2]
    head_dim = query_grid.shape[3]
    place = jnp.arange(span, dtype=jnp.int32)
    valid = (place[None, :] < lengths[:, None])[:, None, None, :]
    scores = jnp.einsum(
        "rqhd,rkhd->rqhk",
        query_grid,
        key_table.reshape(count, span, heads, head_dim),
        preferred_element_type=jnp.float32,
    ) * (1.0 / math.sqrt(head_dim))
    return (jnp.where(valid, scores, NEG), valid)


def prefix_weighted(scores, valid, peaks, value_table, heads, head_dim):
    group_count, span, width = value_table.shape
    weights = jnp.where(valid, jnp.exp(scores - peaks[..., None]), 0.0)
    numer = jnp.einsum(
        "rqhk,khd->rqhd",
        weights.astype(jnp.bfloat16),
        value_table.reshape(group_count * span, heads, head_dim),
        preferred_element_type=jnp.float32,
    )
    return (jnp.sum(weights, axis=-1), numer)


def suffix_weighted(scores, valid, peaks, value_table, heads, head_dim):
    count, span, width = value_table.shape
    weights = jnp.where(valid, jnp.exp(scores - peaks[..., None]), 0.0)
    numer = jnp.einsum(
        "rqhk,rkhd->rqhd",
        weights.astype(jnp.bfloat16),
        value_table.reshape(count, span, heads, head_dim),
        preferred_element_type=jnp.float32,
    )
    return (jnp.sum(weights, axis=-1), numer)


def body(
    token_ids,
    group_ids,
    prefix_lengths,
    cached_lengths,
    embedding,
    ln_gains,
    qkv_weight,
    out_weight,
    up_weight,
    down_weight,
    prefix_keys,
    prefix_values,
    suffix_keys,
    suffix_values,
    final_gain,
    head_weight,
):
    narrow_count = lax.axis_size("narrow")
    narrow_index = lax.axis_index("narrow")
    tok_local = token_ids.shape[0]
    req_total = group_ids.shape[0]
    req_local = req_total // narrow_count
    stretch = tok_local // req_local
    head_dim = HD
    heads_here = qkv_weight.shape[1] // (3 * head_dim)
    width = heads_here * head_dim
    scale = 1.0 / math.sqrt(head_dim)
    all_ids = lax.all_gather(token_ids, "narrow", axis=0, tiled=True)
    vocab_rows = embedding.shape[0]
    local_ids = all_ids - narrow_index * vocab_rows
    inside = (local_ids >= 0) & (local_ids < vocab_rows)
    rows = jnp.take(embedding, jnp.clip(local_ids, 0, vocab_rows - 1), axis=0)
    resid = lax.psum_scatter(
        jnp.where(inside[:, None], rows.astype(jnp.float32), 0.0).astype(jnp.bfloat16),
        "narrow",
        scatter_dimension=0,
        tiled=True,
    )
    whole = lax.all_gather(resid, "wide", axis=1, tiled=True)
    norm_attn = layer_norm(whole, ln_gains[0]).astype(jnp.bfloat16)
    norm_mlp = layer_norm(whole, ln_gains[1]).astype(jnp.bfloat16)
    qkv = add_rows(norm_attn, lax.all_gather(qkv_weight, "narrow", axis=0, tiled=True)).astype(
        jnp.bfloat16
    )
    qkv = qkv.reshape(tok_local, heads_here, 3, head_dim)
    local_pos = jnp.arange(tok_local, dtype=jnp.int32)
    my_requests = narrow_index * req_local + local_pos // stretch
    my_groups = pick(group_ids, my_requests)
    places = (
        pick(prefix_lengths, my_groups) + pick(cached_lengths, my_requests) + local_pos % stretch
    ).astype(jnp.float32)
    queries = rotate(qkv[:, :, 0].astype(jnp.float32), places).astype(jnp.bfloat16)
    keys = rotate(qkv[:, :, 1].astype(jnp.float32), places).astype(jnp.bfloat16)
    values = qkv[:, :, 2]
    own_grid = queries.reshape(req_local, stretch, heads_here, head_dim)
    own_requests = narrow_index * req_local + jnp.arange(req_local, dtype=jnp.int32)
    own_groups = pick(group_ids, own_requests)
    own_cached = pick(cached_lengths, own_requests)
    prefix_all, prefix_vals_all = (
        lax.all_gather(prefix_keys, "narrow", axis=1, tiled=True),
        lax.all_gather(prefix_values, "narrow", axis=1, tiled=True),
    )
    pre_scores, pre_ok = prefix_grid(own_grid, prefix_all, prefix_lengths, own_groups)
    suf_scores, suf_ok = suffix_grid(own_grid, suffix_keys, own_cached)
    far_max = jnp.maximum(jnp.max(pre_scores, axis=-1), jnp.max(suf_scores, axis=-1))
    pre_total, pre_numer = prefix_weighted(
        pre_scores, pre_ok, far_max, prefix_vals_all, heads_here, head_dim
    )
    suf_total, suf_numer = suffix_weighted(
        suf_scores, suf_ok, far_max, suffix_values, heads_here, head_dim
    )
    far_total = pre_total + suf_total
    far_numer = pre_numer + suf_numer
    far_max = far_max.reshape(tok_local, heads_here)
    far_total = far_total.reshape(tok_local, heads_here)
    far_numer = far_numer.reshape(tok_local, heads_here, head_dim)
    local_k = keys.reshape(req_local, stretch, heads_here, head_dim)
    local_v = values.reshape(req_local, stretch, heads_here, head_dim)
    causal = (jnp.arange(stretch)[:, None] >= jnp.arange(stretch)[None, :])[None, :, None, :]
    near_scores = (
        jnp.einsum("rqhd,rkhd->rqhk", own_grid, local_k, preferred_element_type=jnp.float32) * scale
    )
    near_scores = jnp.where(causal, near_scores, NEG)
    near_max = jnp.max(near_scores, axis=-1)
    near_exp = jnp.where(causal, jnp.exp(near_scores - near_max[..., None]), 0.0)
    near_total = jnp.sum(near_exp, axis=-1).reshape(tok_local, heads_here)
    near_numer = jnp.einsum(
        "rqhk,rkhd->rqhd",
        near_exp.astype(jnp.bfloat16),
        local_v,
        preferred_element_type=jnp.float32,
    ).reshape(tok_local, heads_here, head_dim)
    near_max = near_max.reshape(tok_local, heads_here)
    top = jnp.maximum(far_max, near_max)
    far_scale = jnp.exp(far_max - top)
    near_scale = jnp.exp(near_max - top)
    numer = far_numer * far_scale[..., None] + near_numer * near_scale[..., None]
    denom = far_total * far_scale + near_total * near_scale
    attn = (numer / denom[..., None]).reshape(tok_local, width).astype(jnp.bfloat16)
    attn_terms = jnp.dot(
        attn,
        lax.all_gather(out_weight, "narrow", axis=1, tiled=True),
        preferred_element_type=jnp.float32,
    )
    up = add_rows(norm_mlp, lax.all_gather(up_weight, "narrow", axis=0, tiled=True))
    hidden = jax.nn.gelu(up, approximate=False).astype(jnp.bfloat16)
    mlp_terms = jnp.dot(
        hidden,
        lax.all_gather(down_weight, "narrow", axis=1, tiled=True),
        preferred_element_type=jnp.float32,
    )
    layer_sum = lax.psum_scatter(
        (attn_terms + mlp_terms).astype(jnp.bfloat16), "wide", scatter_dimension=1, tiled=True
    ).astype(jnp.float32)
    hidden_out = (resid.astype(jnp.float32) + layer_sum).astype(jnp.bfloat16)
    last_local = hidden_out.reshape(req_local, stretch, hidden_out.shape[1])[:, stretch - 1, :]
    last_wide = lax.all_gather(last_local, "wide", axis=1, tiled=True)
    last_all = lax.all_gather(last_wide, "narrow", axis=0, tiled=True)
    last_values = last_all.astype(jnp.float32)
    last_rms = jnp.sqrt(jnp.mean(last_values * last_values, axis=-1))
    final_rows = layer_norm(last_all, final_gain).astype(jnp.bfloat16)
    logits = jnp.dot(final_rows, head_weight, preferred_element_type=jnp.float32)
    max_logit = lax.pmax(jnp.max(logits, axis=-1), ("wide", "narrow"))
    return (hidden_out, last_rms, max_logit)


def solution(mesh):
    return jax.shard_map(
        body,
        mesh=mesh,
        in_specs=(
            P("narrow"),
            P(),
            P(),
            P(),
            P("narrow", "wide"),
            P(),
            P("narrow", "wide"),
            P("wide", "narrow"),
            P("narrow", "wide"),
            P("wide", "narrow"),
            P(None, "narrow", "wide"),
            P(None, "narrow", "wide"),
            P("narrow", None, "wide"),
            P("narrow", None, "wide"),
            P(),
            P(None, ("wide", "narrow")),
        ),
        out_specs=(P("narrow", "wide"), P(), P()),
        check_vma=False,
    )
```

profile of v0, /device:TPU:1, one launch (start us, length us, event | category | flops | bytes accessed | tf_op | source)
XLA Modules:
  0.0 768.9 jit_solution(16040409166569991938)
XLA Ops:
  7.2 27.0 %all-gather.2 = s32[8,1,512]{2,1,0:T(1,128)S(1)} all-gather(s32[1,1,512]{2,1,0:T(1,128)} %bitcast.193), channel_id=1, replica_groups=mesh['wide'=16,'narrow'=8] {'narrow'}, dimensions={0}, use_global_device_ids=true | all-gather | bytes 18432 | tf_op jit(solution)/shard_map/all_gather | solution.py:128
  34.4 18.2 %gather_fusion = bf16[4096,256]{1,0:T(8,128)(2,1)} fusion(bf16[6304,256]{1,0:T(8,128)(2,1)} %param.20, s32[4096]{0:T(1024)S(1)} %fusion.119), kind=kCustom, calls=%fused_computation | custom fusion | bytes 4210688 | tf_op jit(solution)/shard_map/jit(_take)/gather | solution.py:132
  52.6 5.8 select_convert_fusion
  58.5 80.1 %reduce-scatter.3.cloned.1.call-done = bf16[512,256]{1,0:T(8,128)(2,1)} async-done(((bf16[4096,256]{1,0:T(8,128)(2,1)}), bf16[512,256]{1,0:T(8,128)(2,1)}) %reduce-scatter.3.cloned.1.call-update) | async-done | bytes 262160 | tf_op jit(solution)/shard_map/reduce_scatter | solution.py:133
  145.3 2.3 copy.65
  148.3 2.2 reshape.332
  151.2 31.3 %all_gather.33 = bf16[2,512,256]{2,1,0:T(8,128)(2,1)} all-gather(bf16[2,64,256]{2,1,0:T(8,128)(2,1)S(1)} %copy-done.13), channel_id=1, replica_groups=mesh['wide'=16,'narrow'=8] {'narrow'}, dimensions={1}, use_global_device_ids=true | all-gather | bytes 589824 | tf_op jit(solution)/shard_map/all_gather | solution.py:160
  184.5 31.4 %all_gather.34 = bf16[2,512,256]{2,1,0:T(8,128)(2,1)} all-gather(bf16[2,64,256]{2,1,0:T(8,128)(2,1)S(1)} %copy-done.14), channel_id=1, replica_groups=mesh['wide'=16,'narrow'=8] {'narrow'}, dimensions={1}, use_global_device_ids=true | all-gather | bytes 589824 | tf_op jit(solution)/shard_map/all_gather | solution.py:161
  215.9 2.0 reshape.366
  218.0 3.1 convert_reduce_fusion
  222.8 60.5 %all-gather.11.cloned.1.call-done = bf16[4096,768]{1,0:T(8,128)(2,1)} async-done(((bf16[512,768]{1,0:T(8,128)(2,1)}), bf16[4096,768]{1,0:T(8,128)(2,1)}) %all-gather.11.cloned.1.call-update) | async-done | bytes 6291472 | tf_op jit(solution)/shard_map/all_gather | solution.py:142
  283.3 8.5 %fusion.53 = bf16[512,768]{1,0:T(8,128)(2,1)} fusion(bf16[4096,768]{1,0:T(8,128)(2,1)} %all-gather.11.cloned.1.call-done, bf16[512,4096]{1,0:T(8,128)(2,1)} %all-gather.9.cloned.1.call-done, f32[4096]{0:T(1024)S(1)} %bitcast.191, f32[512]{0:T(512)S(1)} %add_rsqrt_fusion, f32[512]{0:T(512)S(1)} %broadcast_multiply_fusion), kind=kOutput, calls=%fused_computation.65 | convolution fusion | flops 3232104448 | bytes 11292672 | tf_op jit(solution)/shard_map/dot_general | solution.py:39
  291.9 2.3 copy.52
  312.0 2.4 fusion.9
  314.4 2.1 fusion.56
  319.1 82.9 %all-gather.17.cloned.1.call-done = bf16[1024,4096]{1,0:T(8,128)(2,1)} async-done(((bf16[1024,512]{1,0:T(8,128)(2,1)}), bf16[1024,4096]{1,0:T(8,128)(2,1)}) %all-gather.17.cloned.1.call-update) | async-done | bytes 8388624 | tf_op jit(solution)/shard_map/all_gather | solution.py:209
  402.0 109.9 %all-gather.15.cloned.1.call-done = bf16[4096,1024]{1,0:T(8,128)(2,1)} async-done(((bf16[512,1024]{1,0:T(8,128)(2,1)}), bf16[4096,1024]{1,0:T(8,128)(2,1)}) %all-gather.15.cloned.1.call-update) | async-done | bytes 8388624 | tf_op jit(solution)/shard_map/all_gather | solution.py:205
  511.9 23.8 %fusion.46 = f32[512,4096]{1,0:T(8,128)} fusion(bf16[1024,4096]{1,0:T(8,128)(2,1)} %all-gather.17.cloned.1.call-done, bf16[4096,1024]{1,0:T(8,128)(2,1)} %all-gather.15.cloned.1.call-done, bf16[512,4096]{1,0:T(8,128)(2,1)} %all-gather.9.cloned.1.call-done, f32[4096]{0:T(1024)} %bitcast.190, f32[512]{0:T(512)S(1)} %add_rsqrt_fusion, ...), kind=kOutput, calls=%fused_computation.59 | convolution fusion | flops 8634499072 | bytes 29380608 | tf_op jit(solution)/shard_map/dot_general | solution.py:207
  535.7 32.2 %all-gather.13.cloned.1.call-done = bf16[256,4096]{1,0:T(8,128)(2,1)} async-done(((bf16[256,512]{1,0:T(8,128)(2,1)}), bf16[256,4096]{1,0:T(8,128)(2,1)}) %all-gather.13.cloned.1.call-update) | async-done | bytes 2097168 | tf_op jit(solution)/shard_map/all_gather | solution.py:202
  567.9 7.2 add_convert_fusion
  575.1 65.1 %reduce-scatter.5.cloned.1.call-done = bf16[512,256]{1,0:T(8,128)(2,1)} async-done(((bf16[512,4096]{1,0:T(8,128)(2,1)}), bf16[512,256]{1,0:T(8,128)(2,1)}) %reduce-scatter.5.cloned.1.call-update) | async-done | bytes 262160 | tf_op jit(solution)/shard_map/reduce_scatter | solution.py:212
  641.2 20.1 %all-gather = bf16[1,1,4096]{2,1,0:T(2,128)(2,1)S(1)} all-gather(bf16[1,1,256]{2,1,0:T(2,128)(2,1)S(1)} %slice.75), channel_id=2, replica_groups=mesh['wide'=16,'narrow'=8] {'wide'}, dimensions={2}, use_global_device_ids=true | all-gather | bytes 8704 | tf_op jit(solution)/shard_map/all_gather | solution.py:217
  661.3 27.8 %all-gather.1 = bf16[8,1,4096]{2,1,0:T(2,128)(2,1)S(1)} all-gather(bf16[1,1,4096]{2,1,0:T(2,128)(2,1)S(1)} %all-gather), channel_id=3, replica_groups=mesh['wide'=16,'narrow'=8] {'narrow'}, dimensions={0}, use_global_device_ids=true | all-gather | bytes 73728 | tf_op jit(solution)/shard_map/all_gather | solution.py:218
  691.3 70.8 %pmax.7 = f32[8]{0:T(128)} all-reduce(f32[8]{0:T(128)S(1)} %convolution_reduce_fusion), channel_id=1, replica_groups=mesh['wide'=16,'narrow'=8] {'wide','narrow'}, use_global_device_ids=true, to_apply=%region_19.20 | all-reduce | flops 8 | bytes 64 | tf_op jit(solution)/shard_map/pmax | solution.py:223
  (112 shorter events, 35.6 us)
Async XLA Ops:
  7.2 682.5 %copy-start = (bf16[4096,394]{0,1:T(8,128)(2,1)S(1)}, bf16[4096,394]{0,1:T(8,128)(2,1)}, u32[]{:S(2)}) copy-start(bf16[4096,394]{0,1:T(8,128)(2,1)} %param.31) | copy-start | bytes 9682948
  7.2 131.4 %reduce-scatter.3.cloned.1.call-start = ((), (), s32[]{:S(2)}) async-start(), calls=%async_computation.2 | async-start | bytes 2359296 | tf_op jit(solution)/shard_map/reduce_scatter | solution.py:133
  58.4 83.5 %copy-start.15 = (f32[2,4096]{1,0:T(2,128)S(1)}, f32[2,4096]{1,0:T(2,128)}, u32[]{:S(2)}) copy-start(f32[2,4096]{1,0:T(2,128)} %param.21) | copy-start | bytes 98308
  58.4 84.2 %copy-start.17 = (s32[8]{0:T(128)S(1)}, s32[8]{0:T(128)}, u32[]{:S(2)}) copy-start(s32[8]{0:T(128)} %param.19) | copy-start | bytes 100
  58.4 84.1 %copy-start.18 = (s32[8]{0:T(128)S(1)}, s32[8]{0:T(128)}, u32[]{:S(2)}) copy-start(s32[8]{0:T(128)} %param.17) | copy-start | bytes 100
  58.5 84.9 %copy-start.19 = (s32[2]{0:T(128)S(1)}, s32[2]{0:T(128)}, u32[]{:S(2)}) copy-start(s32[2]{0:T(128)} %param.18) | copy-start | bytes 28
  58.5 159.5 %all-gather.9.cloned.1.call-start = ((), (), s32[]{:S(2)}) async-start(), calls=%async_computation.3 | async-start | bytes 4456448 | tf_op jit(solution)/shard_map/all_gather | solution.py:139
  138.6 144.7 %all-gather.11.cloned.1.call-start = ((), (), s32[]{:S(2)}) async-start(), calls=%async_computation.4 | async-start | bytes 7077888 | tf_op jit(solution)/shard_map/all_gather | solution.py:142
  139.4 262.6 %all-gather.17.cloned.1.call-start = ((), (), s32[]{:S(2)}) async-start(), calls=%async_computation.7 | async-start | bytes 9437184 | tf_op jit(solution)/shard_map/all_gather | solution.py:209
  139.9 372.0 %all-gather.15.cloned.1.call-start = ((), (), s32[]{:S(2)}) async-start(), calls=%async_computation.6 | async-start | bytes 9437184 | tf_op jit(solution)/shard_map/all_gather | solution.py:205
  140.5 427.3 %all-gather.13.cloned.1.call-start = ((), (), s32[]{:S(2)}) async-start(), calls=%async_computation.5 | async-start | bytes 2359296 | tf_op jit(solution)/shard_map/all_gather | solution.py:202
  141.1 499.1 %reduce-scatter.5.cloned.1.call-start = ((), (), s32[]{:S(2)}) async-start(), calls=%async_computation.8 | async-start | bytes 4456448 | tf_op jit(solution)/shard_map/reduce_scatter | solution.py:212
  145.3 5.9 copy-start.13
  147.6 36.9 %copy-start.14 = (bf16[2,64,256]{2,1,0:T(8,128)(2,1)S(1)}, bf16[2,64,256]{2,1,0:T(8,128)(2,1)}, u32[]{:S(2)}) copy-start(bf16[2,64,256]{2,1,0:T(8,128)(2,1)} %param.27) | copy-start | bytes 196612
  218.0 3.6 copy-start.1
  303.1 1.7 copy-start.2
  303.1 1.7 copy-start.7
  303.1 1.7 copy-start.8
  309.5 1.6 copy-start.6
  312.0 2.4 copy-start.10
  316.5 1.2 copy-start.11
  575.1 65.1 %copy-start.9 = (bf16[512,256]{1,0:T(8,128)(2,1)S(1)}, bf16[512,256]{1,0:T(8,128)(2,1)}, u32[]{:S(2)}) copy-start(bf16[512,256]{1,0:T(8,128)(2,1)} %reduce-scatter.3.cloned.1.call-done) | copy-start | bytes 786436
  575.1 114.6 %copy-start.16 = (f32[4096]{0:T(1024)S(1)}, f32[4096]{0:T(1024)}, u32[]{:S(2)}) copy-start(f32[4096]{0:T(1024)} %param.30) | copy-start | bytes 49156
  641.2 48.3 %copy-start.12 = (bf16[512,256]{1,0:T(8,128)(2,1)}, bf16[512,256]{1,0:T(8,128)(2,1)S(1)}, u32[]{:S(2)}) copy-start(bf16[512,256]{1,0:T(8,128)(2,1)S(1)} %add_convert_fusion.1) | copy-start | bytes 786436
  (3 other events, 3.1 us)
Sparse Core Ops, SparseCore 0:
  58.5 80.0 reduce-scatter.2
  140.2 49.2 all-gather.8
  191.8 91.4 all-gather.10
  285.3 116.6 all-gather.16
  404.2 107.6 all-gather.14
  513.9 53.8 all-gather.12
  575.2 64.8 reduce-scatter.4
where the time goes:
time: 770 us; the launch traced here: 769 us
  waiting for transfers between devices  433 us (56%)
  blocking collectives  208 us (27%)
  matrix products  48.9 us (6%)
  local copies, waits for them, and re-layouts  40.2 us (5%)
  other arithmetic  23.8 us (3%)
  between operations  14.5 us (2%)
    all_gather x1, waiting for transfers between devices, body(): lax.all_gather(up_weight, 'narrow', axis=0, tiled=True)  110 us
    all_gather x1, waiting for transfers between devices, body(): lax.all_gather(down_weight, 'narrow', axis=1, tiled=True)  82.9 us
    reduce_scatter x1, waiting for transfers between devices, body(): lax.psum_scatter(jnp.where(inside[:, None], rows.astype(jnp.float32), 0.0...  80.1 us
    pmax x1, blocking collectives, body(): max_logit = lax.pmax(jnp.max(logits, axis=-1), ('wide', 'narrow'))  70.8 us
    reduce_scatter x1, waiting for transfers between devices, body(): lax.psum_scatter((attn_terms + mlp_terms).astype(jnp.bfloat16), 'wide', s...  65.1 us
    all_gather x1, waiting for transfers between devices, body(): lax.all_gather(qkv_weight, 'narrow', axis=0, tiled=True)  60.5 us
    all_gather x1, waiting for transfers between devices, body(): lax.all_gather(out_weight, 'narrow', axis=1, tiled=True)  32.2 us
    all_gather x1, blocking collectives, body(): lax.all_gather(prefix_values, 'narrow', axis=1, tiled=True)  31.4 us
  transfers between devices with their start and end apart: 7, of which 6 were waited for; matrix products, arithmetic and copies ran while one was open for 10% of the time, Pallas kernels for 0%

commit v1 on v0

v1 whole, which is shorter than its diff:
```python
import functools
import math

import jax
import jax.numpy as jnp
from jax import lax
from jax.experimental import pallas as pl
from jax.experimental.pallas import tpu as pltpu
from jax.sharding import PartitionSpec as P

HD = 128
ROT = 32
NEG = -1e30
MESH = pl.DeviceIdType.MESH
NN = 8
NWC = 8
F32 = jnp.float32
BF16 = jnp.bfloat16
VMEM_LIMIT = 67000000


def layer_norm(rows, gain):
    values = rows.astype(F32)
    center = values - jnp.mean(values, axis=-1, keepdims=True)
    spread = jnp.mean(center * center, axis=-1, keepdims=True)
    return center * lax.rsqrt(spread + 1e-05) * gain


def pick(table, index):
    match = index[:, None] == jnp.arange(table.shape[0], dtype=jnp.int32)[None, :]
    return jnp.sum(jnp.where(match, table[None, :], 0), axis=1)


def greet(devices):
    barrier = pltpu.get_barrier_semaphore()
    for device in devices:
        pl.semaphore_signal(barrier, inc=1, device_id=device, device_id_type=MESH)
    pl.semaphore_wait(barrier, len(devices))


def others(axis, count):
    me = lax.axis_index(axis)
    return [{axis: lax.rem(me + d, count)} for d in range(1, count)]


def ids_kernel(ids_ref, out_ref, ssem, rsem, lsem):
    n = lax.axis_index("narrow")
    peers = others("narrow", NN)
    greet(peers)
    local = pltpu.make_async_copy(ids_ref, out_ref.at[n], lsem)
    local.start()
    copies = []
    for d, peer in enumerate(peers):
        copies.append(
            pltpu.make_async_remote_copy(
                src_ref=ids_ref,
                dst_ref=out_ref.at[n],
                send_sem=ssem.at[d],
                recv_sem=rsem.at[d],
                device_id=peer,
                device_id_type=MESH,
            )
        )
        copies[-1].start()
    for d, copy in enumerate(copies):
        copy.wait_send()
        copy.wait_recv()
    local.wait()


def gather_ids(token_ids):
    tile = token_ids.reshape(4, 128)
    out = pl.pallas_call(
        ids_kernel,
        out_shape=jax.ShapeDtypeStruct((NN, 4, 128), jnp.int32),
        in_specs=[pl.BlockSpec(memory_space=pltpu.VMEM)],
        out_specs=pl.BlockSpec(memory_space=pltpu.VMEM),
        scratch_shapes=[
            pltpu.SemaphoreType.DMA((NN - 1,)),
            pltpu.SemaphoreType.DMA((NN - 1,)),
            pltpu.SemaphoreType.DMA,
        ],
        compiler_params=pltpu.CompilerParams(collective_id=0, has_side_effects=True),
    )(tile)
    return out.reshape(-1)


def max_kernel(val_ref, out_ref, near, far, part, ssem, rsem):
    n = lax.axis_index("narrow")
    w = lax.axis_index("wide")
    first = others("narrow", NN)
    second = others("wide", 2 * NWC)
    greet(first + second)

    def spread(src, slots, me, peers, base):
        copies = []
        for d, peer in enumerate(peers):
            copies.append(
                pltpu.make_async_remote_copy(
                    src_ref=src,
                    dst_ref=slots.at[d],
                    send_sem=ssem.at[base + d],
                    recv_sem=rsem.at[base + d],
                    device_id=peer,
                    device_id_type=MESH,
                )
            )
            copies[-1].start()
        for copy in copies:
            copy.wait_recv()
        return copies

    sent = spread(val_ref, near, n, first, 0)
    best = val_ref[...]
    for d in range(NN - 1):
        best = jnp.maximum(best, near[d])
    part[...] = best
    sent += spread(part, far, w, second, NN - 1)
    for d in range(2 * NWC - 1):
        best = jnp.maximum(best, far[d])
    out_ref[...] = best
    for copy in sent:
        copy.wait_send()


def max_over_all(values):
    tile = jnp.broadcast_to(values[:, None], (8, 128))
    out = pl.pallas_call(
        max_kernel,
        out_shape=jax.ShapeDtypeStruct((8, 128), F32),
        in_specs=[pl.BlockSpec(memory_space=pltpu.VMEM)],
        out_specs=pl.BlockSpec(memory_space=pltpu.VMEM),
        scratch_shapes=[
            pltpu.VMEM((NN - 1, 8, 128), F32),
            pltpu.VMEM((2 * NWC - 1, 8, 128), F32),
            pltpu.VMEM((8, 128), F32),
            pltpu.SemaphoreType.DMA((22,)),
            pltpu.SemaphoreType.DMA((22,)),
        ],
        compiler_params=pltpu.CompilerParams(collective_id=2, has_side_effects=True),
    )(tile)
    return out[:, 0]


class Spread:
    def __init__(self, own, buf, base, ssem, rsem, lsem, z_first):
        self.own, self.buf, self.base, self.z_first = own, buf, base, z_first
        self.ssem, self.rsem, self.lsem = ssem, rsem, lsem
        n = lax.axis_index("narrow")
        self.n = n
        self.right, self.left = lax.rem(n + 2, NN), lax.rem(n + 6, NN)
        self.far = lax.rem(n + 4, NN)
        self.half = buf.shape[1] // 2
        self.pending = []

    def flip(self, m):
        return m + 1 - 2 * lax.rem(m, 2)

    def part(self, m, h):
        if h is None:
            return self.buf.at[m]
        return self.buf.at[m, pl.ds(h * self.half, self.half)]

    def send(self, i, m, h, dst, src=None):
        copy = pltpu.make_async_remote_copy(
            src_ref=self.part(m, h) if src is None else src,
            dst_ref=self.part(m, h),
            send_sem=self.ssem.at[self.base + i],
            recv_sem=self.rsem.at[self.base + i],
            device_id={"narrow": dst},
            device_id_type=MESH,
        )
        copy.start()
        self.pending.append(copy)

    def arrive(self, i, m, h):
        pltpu.make_async_remote_copy(
            src_ref=self.part(m, h),
            dst_ref=self.part(m, h),
            send_sem=self.ssem.at[self.base + i],
            recv_sem=self.rsem.at[self.base + i],
            device_id={"narrow": self.right},
            device_id_type=MESH,
        ).wait_recv()

    def s0(self):
        n, own = self.n, self.own
        self.local = pltpu.make_async_copy(own, self.buf.at[n], self.lsem)
        self.local.start()
        self.send(0, n, None, self.right, own)
        self.send(1, n, None, self.left, own)
        self.send(2, n, None, self.flip(n), own)

    def s1(self):
        right, left, flip = self.right, self.left, self.flip
        if self.z_first:
            z = flip(self.n)
            self.arrive(2, z, None)
            self.send(3, z, None, right)
            self.send(4, z, None, left)
        self.arrive(0, left, None)
        self.send(5, left, 0, right)
        if not self.z_first:
            self.send(3, left, None, flip(self.n))
        self.arrive(1, right, None)
        self.send(6, right, 1, left)
        if not self.z_first:
            self.send(4, right, None, flip(self.n))

    def s2(self):
        right, left, far, flip = self.right, self.left, self.far, self.flip
        if self.z_first:
            self.arrive(3, flip(left), None)
            self.send(7, flip(left), 0, right)
            self.arrive(4, flip(right), None)
            self.send(8, flip(right), 1, left)
        else:
            self.arrive(5, far, 0)
            self.send(7, far, 0, flip(self.n))
            self.arrive(6, far, 1)
            self.send(8, far, 1, flip(self.n))

    def s3(self):
        right, left, far, flip = self.right, self.left, self.far, self.flip
        if self.z_first:
            self.arrive(5, far, 0)
            self.arrive(6, far, 1)
        else:
            self.arrive(2, flip(self.n), None)
            self.arrive(3, flip(left), None)
            self.arrive(4, flip(right), None)
        self.arrive(7, flip(far), 0)
        self.arrive(8, flip(far), 1)
        self.local.wait()

    def finish(self):
        for copy in self.pending:
            copy.wait_send()


def layer_kernel(
    modes,
    rows,
    wq_in,
    wu_in,
    wd_in,
    wo_in,
    pk_in,
    pv_in,
    sk_in,
    sv_in,
    gains,
    cos_t,
    sin_a,
    sin_b,
    bias,
    out_ref,
    last_ref,
    wq,
    wu,
    wd,
    wo,
    pk,
    pv,
    sk,
    sv,
    emb,
    xs,
    na,
    nm,
    qkv,
    scores,
    probs,
    attn,
    acc,
    hid,
    sib_s,
    sib_r,
    own_s,
    rs_s,
    rs_r,
    last_n,
    last_w,
    ssem,
    rsem,
    lsem,
):
    n = lax.axis_index("narrow")
    w = lax.axis_index("wide")
    c = lax.rem(w, 2)
    wc = lax.div(w, 2)
    sibling = {"wide": w + 1 - 2 * c}
    tokens, feats = out_ref.shape
    scale = 1.0 / math.sqrt(HD)

    def remote(src, dst, i, device):
        return pltpu.make_async_remote_copy(
            src_ref=src,
            dst_ref=dst,
            send_sem=ssem.at[i],
            recv_sem=rsem.at[i],
            device_id=device,
            device_id_type=MESH,
        )

    greet(others("narrow", NN) + others("wide", 2 * NWC))

    names = ["q", "d", "o", "u"]
    spreads = {}
    for k, (name, own, buf) in enumerate(zip(names, (wq_in, wd_in, wo_in, wu_in), (wq, wd, wo, wu))):
        spreads[name] = Spread(own, buf, 9 * k, ssem, rsem, lsem.at[k], modes[name])
    at = 36
    sends = []

    emb_at = at
    at += 7
    own_rows = pltpu.make_async_copy(rows.at[pl.ds(pl.multiple_of(n * tokens, tokens), tokens)], emb.at[n], lsem.at[4])
    own_rows.start()
    for d in range(1, NN):
        m = lax.rem(n + d, NN)
        copy = remote(rows.at[pl.ds(pl.multiple_of(m * tokens, tokens), tokens)], emb.at[n], emb_at + d - 1, {"narrow": m})
        copy.start()
        sends.append(copy)
    spreads["q"].s0()
    pre_at = at
    at += 14
    local_kv = []
    for j, (src, dst) in enumerate(((pk_in, pk), (pv_in, pv))):
        local_kv.append(pltpu.make_async_copy(src.at[n], dst.at[n], lsem.at[5 + j]))
        local_kv[-1].start()
        for d in range(1, NN):
            m = lax.rem(n + d, NN)
            copy = remote(src.at[m], dst.at[n], pre_at + 7 * j + d - 1, {"narrow": m})
            copy.start()
            sends.append(copy)
    for j, (src, dst) in enumerate(((sk_in, sk), (sv_in, sv))):
        local_kv.append(pltpu.make_async_copy(src.at[0], dst, lsem.at[7 + j]))
        local_kv[-1].start()

    own_rows.wait()
    for d in range(1, NN):
        src = lax.rem(n + NN - d, NN)
        remote(emb.at[src], emb.at[src], emb_at + d - 1, sibling).wait_recv()

    @pl.loop(0, tokens // 64)
    def _(i):
        r = pl.ds(pl.multiple_of(i * 64, 64), 64)
        total = emb[0, r, :].astype(F32)
        for m in range(1, NN):
            total = total + emb[m, r, :].astype(F32)
        xs[w, r, :] = total.astype(BF16)

    wide_at = at
    at += 7
    sib_at = at
    at += 8
    for d in range(1, NWC):
        m = lax.rem(wc + d, NWC)
        copy = remote(xs.at[w], xs.at[w], wide_at + d - 1, {"wide": 2 * m + c})
        copy.start()
        sends.append(copy)
    copy = remote(xs.at[w], xs.at[w], sib_at, sibling)
    copy.start()
    sends.append(copy)
    spreads["q"].s1()
    spreads["d"].s0()
    for d in range(1, NWC):
        src = 2 * lax.rem(wc + NWC - d, NWC) + c
        remote(xs.at[src], xs.at[src], wide_at + d - 1, sibling).wait_recv()
        copy = remote(xs.at[src], xs.at[src], sib_at + d, sibling)
        copy.start()
        sends.append(copy)
    spreads["q"].s2()
    spreads["o"].s0()
    spreads["u"].s0()
    spreads["d"].s1()
    for d in range(NWC):
        src = 2 * lax.rem(wc + NWC - d, NWC) + 1 - c
        remote(xs.at[src], xs.at[src], sib_at + d, sibling).wait_recv()

    wide = 2 * NWC
    total_feats = wide * feats

    @pl.loop(0, tokens // 32)
    def _(i):
        r = pl.ds(pl.multiple_of(i * 32, 32), 32)
        total = xs[0, r, :].astype(F32)
        for m in range(1, wide):
            total = total + xs[m, r, :].astype(F32)
        mean = jnp.sum(total, axis=-1, keepdims=True) * (1.0 / total_feats)
        var = jnp.zeros_like(total)
        for m in range(wide):
            center = xs[m, r, :].astype(F32) - mean
            var = var + center * center
        inv = lax.rsqrt(jnp.sum(var, axis=-1, keepdims=True) * (1.0 / total_feats) + 1e-05)
        for m in range(wide):
            cols = slice(m * feats, (m + 1) * feats)
            normed = (xs[m, r, :].astype(F32) - mean) * inv
            na[r, cols] = (normed * gains[0:1, cols]).astype(BF16)
            nm[r, cols] = (normed * gains[1:2, cols]).astype(BF16)

    spreads["q"].s3()

    @pl.loop(0, wq.shape[2] // 256)
    def _(j):
        cols = pl.ds(pl.multiple_of(j * 256, 256), 256)
        weight = wq[:, :, cols].reshape(na.shape[1], 256)
        qkv[:, cols] = jnp.dot(na[...], weight, preferred_element_type=F32).astype(BF16)

    spreads["d"].s2()
    spreads["o"].s1()

    @pl.loop(0, 4)
    def _(i):
        r = pl.ds(pl.multiple_of(i * 128, 128), 128)
        for h in range(2):
            for t in range(2):
                cols = slice((3 * h + t) * HD, (3 * h + t + 1) * HD)
                v = qkv[r, cols].astype(F32)
                turned = v * cos_t[r, :] + pltpu.roll(v, HD - ROT // 2, 1) * sin_a[r, :] + pltpu.roll(v, ROT // 2, 1) * sin_b[r, :]
                qkv[r, cols] = turned.astype(BF16)

    for copy in local_kv:
        copy.wait()
    for j, dst in enumerate((pk, pv)):
        for d in range(1, NN):
            src = lax.rem(n + NN - d, NN)
            remote(dst.at[src], dst.at[src], pre_at + 7 * j + d - 1, sibling).wait_recv()

    pre_len = pk.shape[0] * pk.shape[1]
    suf_len = sk.shape[0]
    qc = scores.shape[0]

    def attend(h):
        hc = slice(h * HD, (h + 1) * HD)
        q_cols = slice(3 * h * HD, (3 * h + 1) * HD)
        k_cols = slice((3 * h + 1) * HD, (3 * h + 2) * HD)
        v_cols = slice((3 * h + 2) * HD, (3 * h + 3) * HD)

        @pl.loop(0, tokens // qc)
        def _(i):
            r = pl.ds(pl.multiple_of(i * qc, qc), qc)
            q = qkv[r, q_cols]

            def score(keys):
                return lax.dot_general(q, keys, (((1,), (1,)), ((), ())), preferred_element_type=F32) * scale

            keys = pk[:, :, hc].reshape(pre_len, HD)
            s = score(keys) + bias[0:1, 0:pre_len]
            scores[:, 0:pre_len] = s
            top = jnp.max(s, axis=-1, keepdims=True)
            for b in range(suf_len // 512):
                lo = pre_len + b * 512
                s = score(sk[b * 512 : (b + 1) * 512, hc]) + bias[0:1, lo : lo + 512]
                scores[:, lo : lo + 512] = s
                top = jnp.maximum(top, jnp.max(s, axis=-1, keepdims=True))
            lo = pre_len + suf_len
            s = score(qkv[:, k_cols])
            row = lax.broadcasted_iota(jnp.int32, s.shape, 0) + i * qc
            col = lax.broadcasted_iota(jnp.int32, s.shape, 1)
            s = jnp.where(row >= col, s, NEG)
            scores[:, lo : lo + tokens] = s
            top = jnp.maximum(top, jnp.max(s, axis=-1, keepdims=True))
            den = jnp.zeros((qc, 1), F32)
            for b in range(scores.shape[1] // 512):
                p = jnp.exp(scores[:, b * 512 : (b + 1) * 512] - top)
                den = den + jnp.sum(p, axis=-1, keepdims=True)
                probs[:, b * 512 : (b + 1) * 512] = p.astype(BF16)
            num = jnp.dot(probs[:, 0:pre_len], pv[:, :, hc].reshape(pre_len, HD), preferred_element_type=F32)
            num = num + jnp.dot(probs[:, pre_len:lo], sv[:, hc], preferred_element_type=F32)
            num = num + jnp.dot(probs[:, lo : lo + tokens], qkv[:, v_cols], preferred_element_type=F32)
            attn[r, hc] = (num / den).astype(BF16)

    attend(0)
    spreads["u"].s1()
    attend(1)
    spreads["o"].s2()
    spreads["u"].s2()

    def up_rows(m, fresh):
        k = pl.ds(pl.multiple_of(m * wu.shape[1], wu.shape[1]), wu.shape[1])

        @pl.loop(0, wu.shape[2] // 256)
        def _(j):
            cols = pl.ds(pl.multiple_of(j * 256, 256), 256)
            part = jnp.dot(nm[:, k], wu[m, :, cols], preferred_element_type=F32)
            if fresh:
                acc[:, cols] = part
            else:
                acc[:, cols] += part

    su = spreads["u"]
    if su.z_first:
        su.local.wait()
        early = [su.flip(n), su.right, su.left, su.flip(su.right), su.flip(su.left)]
        late = [su.far, su.flip(su.far)]
        up_rows(n, True)
        for m in early:
            up_rows(m, False)
        su.arrive(5, su.far, 0)
        su.arrive(6, su.far, 1)
        up_rows(su.far, False)
        su.arrive(7, su.flip(su.far), 0)
        su.arrive(8, su.flip(su.far), 1)
        up_rows(su.flip(su.far), False)
    else:
        su.s3()
        up_rows(0, True)
        for m in range(1, NN):
            up_rows(m, False)

    @pl.loop(0, tokens // 64)
    def _(i):
        r = pl.ds(pl.multiple_of(i * 64, 64), 64)
        u = acc[r, :]
        hid[r, :] = (0.5 * u * (1.0 + lax.erf(u * math.sqrt(0.5)))).astype(BF16)

    spreads["d"].s3()
    spreads["o"].s3()

    pair_at = at
    at += 8
    rs_at = at
    at += 8

    def pair(r):
        return remote(sib_s.at[r], sib_r.at[r], pair_at + r, sibling)

    def chip(r, m):
        return remote(rs_s.at[r], rs_r.at[wc], rs_at + r, {"wide": 2 * m + c})

    def column(r):
        return lax.rem(wc + 1 + r, NWC)

    def terms(m, side):
        cols = pl.ds(pl.multiple_of(side * feats, feats), feats)
        return jnp.dot(hid[...], wd[m, :, cols], preferred_element_type=F32) + jnp.dot(
            attn[...], wo[m, :, cols], preferred_element_type=F32
        )

    def forward(r):
        pair(r).wait_recv()
        rs_s[r] = (own_s[r].astype(F32) + sib_r[r].astype(F32)).astype(BF16)
        chip(r, column(r)).start()

    @pl.loop(0, NWC)
    def _(r):
        m = column(r)
        sib_s[r] = terms(m, 1 - c).astype(BF16)
        pair(r).start()
        own_s[r] = terms(m, c).astype(BF16)

        @pl.when(r >= 1)
        def _():
            forward(r - 1)

    last = NWC - 1
    pair(last).wait_recv()
    for r in range(last):
        src = lax.rem(wc + NWC - 1 - r, NWC)
        remote(rs_r.at[src], rs_r.at[src], rs_at + r, sibling).wait_recv()
    rs_r[wc] = jnp.zeros((tokens, feats), BF16)

    @pl.loop(0, tokens // 64)
    def _(i):
        r = pl.ds(pl.multiple_of(i * 64, 64), 64)
        total = own_s[last, r, :].astype(F32) + sib_r[last, r, :].astype(F32)
        for m in range(NWC):
            total = total + rs_r[m, r, :].astype(F32)
        out_ref[r, :] = (xs[w, r, :].astype(F32) + total).astype(BF16)

    tail = out_ref[tokens - 16 : tokens, :].astype(F32)
    last_n[n] = jnp.broadcast_to(tail[15:16, :], (8, feats))
    ln_at = at
    at += 7
    for d in range(1, NN):
        copy = remote(last_n.at[n], last_n.at[n], ln_at + d - 1, {"narrow": lax.rem(n + d, NN)})
        copy.start()
        sends.append(copy)
    for d in range(1, NN):
        src = lax.rem(n + NN - d, NN)
        remote(last_n.at[src], last_n.at[src], ln_at + d - 1, sibling).wait_recv()
    pick_row = lax.broadcasted_iota(jnp.int32, (8, feats), 0)
    eight = last_n[0]
    for m in range(1, NN):
        eight = jnp.where(pick_row == m, last_n[m], eight)
    last_w[w] = eight
    lw_at = at
    at += 15
    for d in range(1, wide):
        copy = remote(last_w.at[w], last_w.at[w], lw_at + d - 1, {"wide": lax.rem(w + d, wide)})
        copy.start()
        sends.append(copy)
    for d in range(1, wide):
        src = lax.rem(w + wide - d, wide)
        remote(last_w.at[src], last_w.at[src], lw_at + d - 1, sibling).wait_recv()
    for m in range(wide):
        last_ref[:, m * feats : (m + 1) * feats] = last_w[m]

    for copy in sends:
        copy.wait_send()
    for name in names:
        spreads[name].finish()
    for r in range(NWC):
        pair(r).wait_send()
    for r in range(last):
        chip(r, column(r)).wait_send()


def layer(rows, wq, wu, wd, wo, pk, pv, sk, sv, gains, cos_t, sin_a, sin_b, bias):
    tokens = rows.shape[0] // NN
    feats = rows.shape[1]
    dim = 2 * NWC * feats
    keys = bias.shape[1]
    qc = 256
    vm = pltpu.VMEM
    anywhere = pl.BlockSpec(memory_space=pl.ANY)
    inside = pl.BlockSpec(memory_space=pltpu.VMEM)
    modes = {"q": True, "d": True, "o": True, "u": True}
    blocks = (NWC, tokens, feats)
    return pl.pallas_call(
        functools.partial(layer_kernel, modes),
        out_shape=(
            jax.ShapeDtypeStruct((tokens, feats), BF16),
            jax.ShapeDtypeStruct((NN, dim), F32),
        ),
        in_specs=[anywhere] * 9 + [inside] * 5,
        out_specs=(inside, inside),
        scratch_shapes=[
            vm((NN,) + wq.shape, BF16),
            vm((NN,) + wu.shape, BF16),
            vm((NN,) + wd.shape, BF16),
            vm((NN,) + wo.shape, BF16),
            vm(pk.shape, BF16),
            vm(pv.shape, BF16),
            vm(sk.shape[1:], BF16),
            vm(sv.shape[1:], BF16),
            vm((NN, tokens, feats), BF16),
            vm((2 * NWC, tokens, feats), BF16),
            vm((tokens, dim), BF16),
            vm((tokens, dim), BF16),
            vm((tokens, wq.shape[1]), BF16),
            vm((qc, keys), F32),
            vm((qc, keys), BF16),
            vm((tokens, feats), BF16),
            vm((tokens, wu.shape[1]), F32),
            vm((tokens, wu.shape[1]), BF16),
            vm(blocks, BF16),
            vm(blocks, BF16),
            vm(blocks, BF16),
            vm((NWC - 1, tokens, feats), BF16),
            vm(blocks, BF16),
            vm((NN, 8, feats), F32),
            vm((2 * NWC, 8, feats), F32),
            pltpu.SemaphoreType.DMA((112,)),
            pltpu.SemaphoreType.DMA((112,)),
            pltpu.SemaphoreType.DMA((9,)),
        ],
        compiler_params=pltpu.CompilerParams(
            collective_id=1, has_side_effects=True, vmem_limit_bytes=VMEM_LIMIT
        ),
    )(rows, wq, wu, wd, wo, pk, pv, sk, sv, gains, cos_t, sin_a, sin_b, bias)


def body(
    token_ids,
    group_ids,
    prefix_lengths,
    cached_lengths,
    embedding,
    ln_gains,
    qkv_weight,
    out_weight,
    up_weight,
    down_weight,
    prefix_keys,
    prefix_values,
    suffix_keys,
    suffix_values,
    final_gain,
    head_weight,
):
    n = lax.axis_index("narrow")
    stretch = token_ids.shape[0]
    all_ids = gather_ids(token_ids)
    vocab_rows = embedding.shape[0]
    local_ids = all_ids - n * vocab_rows
    inside = (local_ids >= 0) & (local_ids < vocab_rows)
    rows = jnp.take(embedding, jnp.clip(local_ids, 0, vocab_rows - 1), axis=0)
    rows = jnp.where(inside[:, None], rows, jnp.zeros((), BF16))

    second = (group_ids == 1)[:, None, None]
    pk = jnp.where(second, prefix_keys[1][None], prefix_keys[0][None])
    pv = jnp.where(second, prefix_values[1][None], prefix_values[0][None])
    me = n[None]
    group = pick(group_ids, me)
    far = pick(prefix_lengths, group)[0]
    cached = pick(cached_lengths, me)[0]
    places = (far + cached + jnp.arange(stretch, dtype=jnp.int32)).astype(F32)
    half = ROT // 2
    freqs = jnp.power(10000.0, -(jnp.arange(half).astype(F32) * 2.0 / ROT))
    angles = places[:, None] * freqs[None, :]
    cosine, sine = jnp.cos(angles), jnp.sin(angles)
    rest = HD - ROT
    cos_t = jnp.concatenate([cosine, cosine, jnp.ones((stretch, rest), F32)], axis=1)
    sin_a = jnp.concatenate([-sine, jnp.zeros((stretch, HD - half), F32)], axis=1)
    sin_b = jnp.concatenate([jnp.zeros((stretch, half), F32), sine, jnp.zeros((stretch, rest), F32)], axis=1)
    pre = NN * prefix_keys.shape[1]
    ok = jnp.concatenate(
        [
            jnp.arange(pre, dtype=jnp.int32) < far,
            jnp.arange(suffix_keys.shape[1], dtype=jnp.int32) < cached,
            jnp.ones((stretch,), bool),
        ]
    )
    bias = jnp.broadcast_to(jnp.where(ok, 0.0, NEG).astype(F32)[None, :], (8, ok.shape[0]))

    hidden_out, last_values = layer(
        rows,
        qkv_weight,
        up_weight,
        down_weight,
        out_weight,
        pk,
        pv,
        suffix_keys,
        suffix_values,
        ln_gains,
        cos_t,
        sin_a,
        sin_b,
        bias,
    )
    last_rms = jnp.sqrt(jnp.mean(last_values * last_values, axis=-1))
    final_rows = layer_norm(last_values, final_gain).astype(BF16)
    logits = jnp.dot(final_rows, head_weight, preferred_element_type=F32)
    max_logit = max_over_all(jnp.max(logits, axis=-1))
    return (hidden_out, last_rms, max_logit)


def solution(mesh):
    return jax.shard_map(
        body,
        mesh=mesh,
        in_specs=(
            P("narrow"),
            P(),
            P(),
            P(),
            P("narrow", "wide"),
            P(),
            P("narrow", "wide"),
            P("wide", "narrow"),
            P("narrow", "wide"),
            P("wide", "narrow"),
            P(None, "narrow", "wide"),
            P(None, "narrow", "wide"),
            P("narrow", None, "wide"),
            P("narrow", None, "wide"),
            P(),
            P(None, ("wide", "narrow")),
        ),
        out_specs=(P("narrow", "wide"), P(), P()),
        check_vma=False,
    )
```

time: 770 us -> 380 us (0.49)
  waiting for transfers between devices: 433 us -> 0 us
  Pallas kernels: 0 us -> 334 us
  blocking collectives: 208 us -> 0 us
  matrix products: 48.9 us -> 3.1 us
  local copies, waits for them, and re-layouts: 40.2 us -> 21.9 us
  between operations: 14.5 us -> 2.07 us
    pallas_call x0 -> x3, Pallas kernels: none -> 334 us  [the longest x1 309 us: layer(): pl.pallas_call(functools.partial(layer_kernel, modes), out_shape=(jax.Sha...]
    all_gather x5 -> x0, waiting for transfers between devices: 286 us -> none  [the longest x1 110 us: body(): lax.all_gather(up_weight, 'narrow', axis=0, tiled=True)]
    reduce_scatter x2 -> x0, waiting for transfers between devices: 145 us -> none  [the longest x1 80.1 us: body(): lax.psum_scatter(jnp.where(inside[:, None], rows.astype(jnp.float32), 0.0...]
    all_gather x5 -> x0, blocking collectives: 138 us -> none  [the longest x1 31.4 us: body(): lax.all_gather(prefix_values, 'narrow', axis=1, tiled=True)]
    pmax x1 -> x0, blocking collectives: 70.8 us -> none  [body(): max_logit = lax.pmax(jnp.max(logits, axis=-1), ('wide', 'narrow'))]
    dot_general x10 -> x1, matrix products: 48.9 us -> 3.1 us  [body(): logits = jnp.dot(final_rows, head_weight, preferred_element_type=F32)]
    convert_element_type x7 -> x1, other arithmetic: 9.01 us -> 0.01 us  [body(): places = (far + cached + jnp.arange(stretch, dtype=jnp.int32)).astype(F32)]
  transfers between devices with their start and end apart: 7 -> 0, of which waited for: 6 -> 0; matrix products, arithmetic and copies ran while one was open for 10% -> 0% of each run, Pallas kernels for 0% -> 0%
where the time goes in v1:
time: 380 us
  Pallas kernels  334 us (88%)
  local copies, waits for them, and re-layouts  21.9 us (6%)
  other arithmetic  19 us (5%)
    pallas_call x1, Pallas kernels, layer(): pl.pallas_call(functools.partial(layer_kernel, modes), out_shape=(jax.Sha...  309 us
    gather x1, local copies, waits for them, and re-layouts, body(): rows = jnp.take(embedding, jnp.clip(local_ids, 0, vocab_rows - 1), axis=0)  16.9 us
    pallas_call x1, Pallas kernels, max_over_all(): pl.pallas_call(max_kernel, out_shape=jax.ShapeDtypeStruct((8, 128), F32),...  14.4 us
    pallas_call x1, Pallas kernels, gather_ids(): pl.pallas_call(ids_kernel, out_shape=jax.ShapeDtypeStruct((NN, 4, 128), j...  10.6 us

profile of v1, /device:TPU:1, one launch (start us, length us, event | category | flops | bytes accessed | tf_op | source)
XLA Modules:
  0.0 379.8 jit_solution(5319229202660282325)
XLA Ops:
  0.6 0.8 broadcast_compare_fusion
  1.6 1.3 fusion.4
  2.9 1.9 fusion.6
  6.2 0.7 iota_compare_fusion.1
  6.8 0.7 iota_compare_fusion
  7.5 10.6 %shard_map.175 = s32[8,4,128]{2,1,0:T(4,128)} custom-call(s32[4,128]{1,0:T(4,128)} %bitcast.18), custom_call_target="tpu_custom_call" | custom-call | tf_op jit(solution)/shard_map/pallas_call | solution.py:73
  18.1 0.7 compare_and_fusion.1
  18.9 0.7 subtract_clamp_fusion
  20.3 0.8 slice_bitcast_fusion.1
  21.1 0.9 broadcast_select_fusion
  22.0 1.0 multiply_sine_fusion
  23.0 0.9 maximum_maximum_fusion.1.sin_b
  23.9 0.8 maximum_maximum_fusion.cos_t
  24.7 0.7 concatenate.17.sin_a
  25.5 16.9 %gather_fusion = bf16[4096,256]{1,0:T(8,128)(2,1)} fusion(bf16[6304,256]{1,0:T(8,128)(2,1)S(1)} %copy-done, s32[4096]{0:T(1024)S(1)} %broadcast_clamp_fusion), kind=kCustom, calls=%fused_computation | custom fusion | bytes 4210688 | tf_op jit(solution)/shard_map/jit(_take)/gather | solution.py:689
  42.4 5.8 %select_select_fusion.rows = bf16[4096,256]{1,0:T(8,128)(2,1)} fusion(bf16[4096,256]{1,0:T(8,128)(2,1)} %gather_fusion, pred[4096]{0:T(1024)(128)(4,1)S(1)} %compare_and_fusion, pred[4096]{0:T(1024)(128)(4,1)S(1)} %bitcast.17), kind=kLoop, calls=%fused_computation.1 | loop fusion | flops 2097152 | bytes 4202496 | tf_op jit(solution)/shard_map/jit(_where)/select_n | solution.py:690
  48.1 308.6 %shard_map.176 = (bf16[512,256]{1,0:T(8,128)(2,1)}, f32[8,4096]{1,0:T(8,128)}) custom-call(bf16[4096,256]{1,0:T(8,128)(2,1)} %select_select_fusion.rows, bf16[512,768]{1,0:T(8,128)(2,1)} %wq_in.1, bf16[512,1024]{1,0:T(8,128)(2,1)} %wu_in.1, bf16[1024,512]{1,0:T(8,128)(2,1)} %wd_in.1, bf16[256,512]{1,0:T(8,128)(2,1)} %wo_in.1, ...), custom_call_target="tpu_custom_call" | custom-call | tf_op jit(solution)/shard_map/pallas_call | solution.py:621
  356.7 1.1 reduce_sum.58
  357.8 1.1 multiply_reduce_fusion
  359.0 3.1 convolution_reduce_fusion
  362.6 0.7 broadcast_in_dim.145.val_ref
  363.3 14.4 %shard_map.177 = f32[8,128]{1,0:T(8,128)} custom-call(f32[8,128]{1,0:T(8,128)} %broadcast_in_dim.145.val_ref), custom_call_target="tpu_custom_call" | custom-call | tf_op jit(solution)/shard_map/pallas_call | solution.py:128
  377.7 1.3 slice_reduce_fusion
  379.1 0.7 copy.21
  (23 shorter events, 1.4 us)
Async XLA Ops:
  0.6 24.8 %copy-start = (bf16[6304,256]{1,0:T(8,128)(2,1)S(1)}, bf16[6304,256]{1,0:T(8,128)(2,1)}, u32[]{:S(2)}) copy-start(bf16[6304,256]{1,0:T(8,128)(2,1)} %param.20) | copy-start | bytes 9682948
  48.1 310.8 %copy-start.2 = (f32[4096]{0:T(1024)S(1)}, f32[4096]{0:T(1024)}, u32[]{:S(2)}) copy-start(f32[4096]{0:T(1024)} %param.30) | copy-start | bytes 49156
  356.7 22.3 %copy-start.1 = (bf16[512,256]{1,0:T(8,128)(2,1)S(1)}, bf16[512,256]{1,0:T(8,128)(2,1)}, u32[]{:S(2)}) copy-start(bf16[512,256]{1,0:T(8,128)(2,1)} %get-tuple-element.25) | copy-start | bytes 786436

commit v2 on v1

--- a/solution.py
+++ b/solution.py
@@ -1,4 +1,3 @@
-import functools
 import math
 
 import jax
@@ -143,103 +142,78 @@
 
 
 class Spread:
-    def __init__(self, own, buf, base, ssem, rsem, lsem, z_first):
-        self.own, self.buf, self.base, self.z_first = own, buf, base, z_first
-        self.ssem, self.rsem, self.lsem = ssem, rsem, lsem
-        n = lax.axis_index("narrow")
-        self.n = n
-        self.right, self.left = lax.rem(n + 2, NN), lax.rem(n + 6, NN)
-        self.far = lax.rem(n + 4, NN)
-        self.half = buf.shape[1] // 2
-        self.pending = []
-
-    def flip(self, m):
-        return m + 1 - 2 * lax.rem(m, 2)
-
-    def part(self, m, h):
-        if h is None:
-            return self.buf.at[m]
-        return self.buf.at[m, pl.ds(h * self.half, self.half)]
-
-    def send(self, i, m, h, dst, src=None):
-        copy = pltpu.make_async_remote_copy(
-            src_ref=self.part(m, h) if src is None else src,
-            dst_ref=self.part(m, h),
+    def __init__(self, own, buf, base, sems, place):
+        self.own, self.buf, self.base = own, buf, base
+        self.ssem, self.rsem, self.lsem = sems
+        self.n, self.w, self.x, self.c, self.home, self.away, self.swap, self.sibling = place
+        self.first = 2 * self.x + self.c
+        self.arrivals = [lax.rem(self.first + NN - d, NN) for d in (2, 6, 4)]
+
+    def copy(self, i, src, m, dst):
+        return pltpu.make_async_remote_copy(
+            src_ref=src,
+            dst_ref=self.buf.at[m],
             send_sem=self.ssem.at[self.base + i],
             recv_sem=self.rsem.at[self.base + i],
-            device_id={"narrow": dst},
+            device_id=dst,
             device_id_type=MESH,
         )
-        copy.start()
-        self.pending.append(copy)
-
-    def arrive(self, i, m, h):
-        pltpu.make_async_remote_copy(
-            src_ref=self.part(m, h),
-            dst_ref=self.part(m, h),
-            send_sem=self.ssem.at[self.base + i],
-            recv_sem=self.rsem.at[self.base + i],
-            device_id={"narrow": self.right},
-            device_id_type=MESH,
-        ).wait_recv()
-
-    def s0(self):
-        n, own = self.n, self.own
-        self.local = pltpu.make_async_copy(own, self.buf.at[n], self.lsem)
-        self.local.start()
-        self.send(0, n, None, self.right, own)
-        self.send(1, n, None, self.left, own)
-        self.send(2, n, None, self.flip(n), own)
-
-    def s1(self):
-        right, left, flip = self.right, self.left, self.flip
-        if self.z_first:
-            z = flip(self.n)
-            self.arrive(2, z, None)
-            self.send(3, z, None, right)
-            self.send(4, z, None, left)
-        self.arrive(0, left, None)
-        self.send(5, left, 0, right)
-        if not self.z_first:
-            self.send(3, left, None, flip(self.n))
-        self.arrive(1, right, None)
-        self.send(6, right, 1, left)
-        if not self.z_first:
-            self.send(4, right, None, flip(self.n))
-
-    def s2(self):
-        right, left, far, flip = self.right, self.left, self.far, self.flip
-        if self.z_first:
-            self.arrive(3, flip(left), None)
-            self.send(7, flip(left), 0, right)
-            self.arrive(4, flip(right), None)
-            self.send(8, flip(right), 1, left)
-        else:
-            self.arrive(5, far, 0)
-            self.send(7, far, 0, flip(self.n))
-            self.arrive(6, far, 1)
-            self.send(8, far, 1, flip(self.n))
-
-    def s3(self):
-        right, left, far, flip = self.right, self.left, self.far, self.flip
-        if self.z_first:
-            self.arrive(5, far, 0)
-            self.arrive(6, far, 1)
-        else:
-            self.arrive(2, flip(self.n), None)
-            self.arrive(3, flip(left), None)
-            self.arrive(4, flip(right), None)
-        self.arrive(7, flip(far), 0)
-        self.arrive(8, flip(far), 1)
-        self.local.wait()
+
+    def fan(self, src):
+        for i, d in enumerate((2, 6, 4)):
+            self.copy(i, src, self.first, {"narrow": lax.rem(self.n + d, NN)}).start()
+        self.copy(3, src, self.first, self.sibling).start()
+
+    def local(self):
+        return pltpu.make_async_copy(self.own, self.buf.at[self.n], self.lsem)
+
+    def z(self):
+        return self.copy(7, self.own, self.n, self.swap)
+
+    def start_home(self):
+        @pl.when(self.home)
+        def _():
+            self.local().start()
+            self.fan(self.own)
+
+    def start_away(self):
+        @pl.when(self.away)
+        def _():
+            self.z().start()
+
+    def relay(self):
+        @pl.when(self.away)
+        def _():
+            self.copy(7, self.own, self.first, self.swap).wait_recv()
+            self.fan(self.buf.at[self.first])
+
+        @pl.when(self.home)
+        def _():
+            self.local().wait()
+
+    def share(self):
+        for i, m in enumerate(self.arrivals):
+            self.copy(i, self.buf.at[m], m, self.sibling).wait_recv()
+            self.copy(4 + i, self.buf.at[m], m, self.sibling).start()
+
+    def others(self):
+        flip = 1 - 2 * self.c
+        return [self.first + flip] + [m + flip for m in self.arrivals]
+
+    def complete(self):
+        for i, m in enumerate(self.others()):
+            self.copy(3 + i, self.buf.at[m], m, self.sibling).wait_recv()
 
     def finish(self):
-        for copy in self.pending:
-            copy.wait_send()
+        for i in range(7):
+            self.copy(i, self.buf.at[self.first], self.first, self.sibling).wait_send()
+
+        @pl.when(self.away)
+        def _():
+            self.z().wait_send()
 
 
 def layer_kernel(
-    modes,
     rows,
     wq_in,
     wu_in,
@@ -249,6 +223,7 @@
     pv_in,
     sk_in,
     sv_in,
+    owner,
     gains,
     cos_t,
     sin_a,
@@ -265,6 +240,7 @@
     sk,
     sv,
     emb,
+    resid,
     xs,
     na,
     nm,
@@ -274,11 +250,10 @@
     attn,
     acc,
     hid,
-    sib_s,
-    sib_r,
-    own_s,
-    rs_s,
-    rs_r,
+    ry_s,
+    ry_r,
+    rz_s,
+    rz_r,
     last_n,
     last_w,
     ssem,
@@ -289,27 +264,44 @@
     w = lax.axis_index("wide")
     c = lax.rem(w, 2)
     wc = lax.div(w, 2)
-    sibling = {"wide": w + 1 - 2 * c}
+    y, zl = lax.div(wc, 2), lax.rem(wc, 2)
+    x, zh = lax.div(n, 2), lax.rem(n, 2)
+    home, away = zh == c, zh != c
+    n_flip, w_flip = n + 1 - 2 * zh, w + 1 - 2 * c
+    sibling = {"wide": w_flip}
+    swap = {"narrow": n_flip, "wide": w_flip}
     tokens, feats = out_ref.shape
     scale = 1.0 / math.sqrt(HD)
-
-    def remote(src, dst, i, device):
+    wide = 2 * NWC
+
+    def remote(src, dst, i, device, j=None):
         return pltpu.make_async_remote_copy(
             src_ref=src,
             dst_ref=dst,
             send_sem=ssem.at[i],
-            recv_sem=rsem.at[i],
+            recv_sem=rsem.at[i if j is None else j],
             device_id=device,
             device_id_type=MESH,
         )
 
-    greet(others("narrow", NN) + others("wide", 2 * NWC))
-
+    greeted = []
+    for d in range(NN):
+        for e in range(2):
+            if d or e:
+                greeted.append({"narrow": lax.rem(n + d, NN), "wide": 2 * wc + lax.rem(c + e, 2)})
+    for d in range(2):
+        for e in range(1, NWC):
+            for f in range(2):
+                greeted.append({"narrow": 2 * x + lax.rem(zh + d, 2), "wide": 2 * lax.rem(wc + e, NWC) + f})
+    greet(greeted)
+
+    place = (n, w, x, c, home, away, swap, sibling)
     names = ["q", "d", "o", "u"]
     spreads = {}
     for k, (name, own, buf) in enumerate(zip(names, (wq_in, wd_in, wo_in, wu_in), (wq, wd, wo, wu))):
-        spreads[name] = Spread(own, buf, 9 * k, ssem, rsem, lsem.at[k], modes[name])
-    at = 36
+        spreads[name] = Spread(own, buf, 8 * k, (ssem, rsem, lsem.at[k]), place)
+    sq, sd, so, su = (spreads[name] for name in names)
+    at = 32
     sends = []
 
     emb_at = at
@@ -321,21 +313,9 @@
         copy = remote(rows.at[pl.ds(pl.multiple_of(m * tokens, tokens), tokens)], emb.at[n], emb_at + d - 1, {"narrow": m})
         copy.start()
         sends.append(copy)
-    spreads["q"].s0()
-    pre_at = at
-    at += 14
-    local_kv = []
-    for j, (src, dst) in enumerate(((pk_in, pk), (pv_in, pv))):
-        local_kv.append(pltpu.make_async_copy(src.at[n], dst.at[n], lsem.at[5 + j]))
-        local_kv[-1].start()
-        for d in range(1, NN):
-            m = lax.rem(n + d, NN)
-            copy = remote(src.at[m], dst.at[n], pre_at + 7 * j + d - 1, {"narrow": m})
-            copy.start()
-            sends.append(copy)
-    for j, (src, dst) in enumerate(((sk_in, sk), (sv_in, sv))):
-        local_kv.append(pltpu.make_async_copy(src.at[0], dst, lsem.at[7 + j]))
-        local_kv[-1].start()
+    sq.start_home()
+    sq.start_away()
+    sd.start_home()
 
     own_rows.wait()
     for d in range(1, NN):
@@ -345,40 +325,101 @@
     @pl.loop(0, tokens // 64)
     def _(i):
         r = pl.ds(pl.multiple_of(i * 64, 64), 64)
-        total = emb[0, r, :].astype(F32)
+        who = owner[r, :]
+        total = emb[0, r, :]
         for m in range(1, NN):
-            total = total + emb[m, r, :].astype(F32)
-        xs[w, r, :] = total.astype(BF16)
-
-    wide_at = at
-    at += 7
-    sib_at = at
-    at += 8
-    for d in range(1, NWC):
-        m = lax.rem(wc + d, NWC)
-        copy = remote(xs.at[w], xs.at[w], wide_at + d - 1, {"wide": 2 * m + c})
-        copy.start()
-        sends.append(copy)
-    copy = remote(xs.at[w], xs.at[w], sib_at, sibling)
-    copy.start()
-    sends.append(copy)
-    spreads["q"].s1()
-    spreads["d"].s0()
-    for d in range(1, NWC):
-        src = 2 * lax.rem(wc + NWC - d, NWC) + c
-        remote(xs.at[src], xs.at[src], wide_at + d - 1, sibling).wait_recv()
-        copy = remote(xs.at[src], xs.at[src], sib_at + d, sibling)
-        copy.start()
-        sends.append(copy)
-    spreads["q"].s2()
-    spreads["o"].s0()
-    spreads["u"].s0()
-    spreads["d"].s1()
-    for d in range(NWC):
-        src = 2 * lax.rem(wc + NWC - d, NWC) + 1 - c
-        remote(xs.at[src], xs.at[src], sib_at + d, sibling).wait_recv()
-
-    wide = 2 * NWC
+            total = jnp.where(who == m, emb[m, r, :], total)
+        resid[r, :] = total
+
+        @pl.when(home)
+        def _():
+            xs[w, r, :] = total
+
+    z_at = at
+    at += 4
+    y_at = at
+    at += 12
+
+    def over_z(d, e):
+        m = {"narrow": 2 * x + lax.rem(zh + d, 2), "wide": (2 * y + lax.rem(zl + e, 2)) * 2 + zh}
+        return remote(resid, xs.at[w], z_at + 2 * d + e, m, z_at + 2 * zl + c)
+
+    for d, e in ((0, 1), (1, 0), (1, 1)):
+        over_z(d, e).start()
+
+    @pl.when(away)
+    def _():
+        over_z(0, 0).start()
+
+    sq.relay()
+    sd.start_away()
+
+    suffix_at = at
+    at += 2
+    suffix = ((sk_in.at[0], sk), (sv_in.at[0], sv))
+
+    @pl.when(home)
+    def _():
+        for j, (src, dst) in enumerate(suffix):
+            pltpu.make_async_copy(src, dst, lsem.at[5 + j]).start()
+
+    @pl.when(away)
+    def _():
+        for j, (src, dst) in enumerate(suffix):
+            remote(src, dst, suffix_at + j, swap).start()
+
+    def over_y(i, d):
+        block = 4 * y + i
+        m = {"wide": (2 * lax.rem(y + d, 4) + zl) * 2 + c}
+        return remote(xs.at[block], xs.at[block], y_at + 4 * (d - 1) + i, m)
+
+    for i in range(4):
+        block = 4 * y + i
+
+        @pl.when(jnp.logical_not(jnp.logical_and(home, 2 * zl + c == i)))
+        def _():
+            remote(xs.at[block], xs.at[block], z_at + i, sibling).wait_recv()
+
+        for d in range(1, 4):
+            over_y(i, d).start()
+
+    pre_at = at
+    at += 16
+    prefix = ((pk_in, pk), (pv_in, pv))
+
+    def over_x(j, d, e):
+        src, dst = prefix[j]
+        px, pc = lax.rem(x + d, 4), lax.rem(c + e, 2)
+        m = {"narrow": 2 * px + c, "wide": 2 * wc + pc}
+        return remote(src.at[2 * px + pc], dst.at[n], pre_at + 8 * j + 2 * d + e, m, pre_at + 8 * j + 4 * zh + d)
+
+    for j in range(2):
+        for d in range(4):
+            for e in range(2):
+                if d or e:
+                    over_x(j, d, e).start()
+
+    @pl.when(home)
+    def _():
+        for j, (src, dst) in enumerate(prefix):
+            pltpu.make_async_copy(src.at[n], dst.at[n], lsem.at[7 + j]).start()
+
+    @pl.when(away)
+    def _():
+        for j in range(2):
+            over_x(j, 0, 0).start()
+
+    so.start_home()
+    so.start_away()
+    su.start_home()
+    su.start_away()
+    sq.share()
+    sd.relay()
+    for i in range(4):
+        for d in range(1, 4):
+            block = 4 * lax.rem(y + 4 - d, 4) + i
+            remote(xs.at[block], xs.at[block], y_at + 4 * (d - 1) + i, sibling).wait_recv()
+
     total_feats = wide * feats
 
     @pl.loop(0, tokens // 32)
@@ -399,7 +440,9 @@
             na[r, cols] = (normed * gains[0:1, cols]).astype(BF16)
             nm[r, cols] = (normed * gains[1:2, cols]).astype(BF16)
 
-    spreads["q"].s3()
+    so.relay()
+    su.relay()
+    sq.complete()
 
     @pl.loop(0, wq.shape[2] // 256)
     def _(j):
@@ -407,8 +450,7 @@
         weight = wq[:, :, cols].reshape(na.shape[1], 256)
         qkv[:, cols] = jnp.dot(na[...], weight, preferred_element_type=F32).astype(BF16)
 
-    spreads["d"].s2()
-    spreads["o"].s1()
+    sd.share()
 
     @pl.loop(0, 4)
     def _(i):
@@ -420,12 +462,33 @@
                 turned = v * cos_t[r, :] + pltpu.roll(v, HD - ROT // 2, 1) * sin_a[r, :] + pltpu.roll(v, ROT // 2, 1) * sin_b[r, :]
                 qkv[r, cols] = turned.astype(BF16)
 
-    for copy in local_kv:
-        copy.wait()
-    for j, dst in enumerate((pk, pv)):
-        for d in range(1, NN):
-            src = lax.rem(n + NN - d, NN)
-            remote(dst.at[src], dst.at[src], pre_at + 7 * j + d - 1, sibling).wait_recv()
+    @pl.when(home)
+    def _():
+        for j, (src, dst) in enumerate(suffix):
+            pltpu.make_async_copy(src, dst, lsem.at[5 + j]).wait()
+
+    @pl.when(away)
+    def _():
+        for j, (src, dst) in enumerate(suffix):
+            remote(src, dst, suffix_at + j, swap).wait_recv()
+
+    for j, (src, dst) in enumerate(prefix):
+        for sz in range(2):
+            for d in range(4):
+                m = 2 * lax.rem(x + 4 - d, 4) + sz
+                arrival = remote(dst.at[m], dst.at[m], pre_at, sibling, pre_at + 8 * j + 4 * sz + d)
+                if d:
+                    arrival.wait_recv()
+                else:
+                    mine = jnp.logical_and(home, zh == sz)
+
+                    @pl.when(mine)
+                    def _():
+                        pltpu.make_async_copy(src.at[n], dst.at[n], lsem.at[7 + j]).wait()
+
+                    @pl.when(jnp.logical_not(mine))
+                    def _():
+                        arrival.wait_recv()
 
     pre_len = pk.shape[0] * pk.shape[1]
     suf_len = sk.shape[0]
@@ -472,10 +535,9 @@
             attn[r, hc] = (num / den).astype(BF16)
 
     attend(0)
-    spreads["u"].s1()
+    so.share()
+    su.share()
     attend(1)
-    spreads["o"].s2()
-    spreads["u"].s2()
 
     def up_rows(m, fresh):
         k = pl.ds(pl.multiple_of(m * wu.shape[1], wu.shape[1]), wu.shape[1])
@@ -489,25 +551,12 @@
             else:
                 acc[:, cols] += part
 
-    su = spreads["u"]
-    if su.z_first:
-        su.local.wait()
-        early = [su.flip(n), su.right, su.left, su.flip(su.right), su.flip(su.left)]
-        late = [su.far, su.flip(su.far)]
-        up_rows(n, True)
-        for m in early:
-            up_rows(m, False)
-        su.arrive(5, su.far, 0)
-        su.arrive(6, su.far, 1)
-        up_rows(su.far, False)
-        su.arrive(7, su.flip(su.far), 0)
-        su.arrive(8, su.flip(su.far), 1)
-        up_rows(su.flip(su.far), False)
-    else:
-        su.s3()
-        up_rows(0, True)
-        for m in range(1, NN):
-            up_rows(m, False)
+    up_rows(su.first, True)
+    for m in su.arrivals:
+        up_rows(m, False)
+    su.complete()
+    for m in su.others():
+        up_rows(m, False)
 
     @pl.loop(0, tokens // 64)
     def _(i):
@@ -515,59 +564,80 @@
         u = acc[r, :]
         hid[r, :] = (0.5 * u * (1.0 + lax.erf(u * math.sqrt(0.5)))).astype(BF16)
 
-    spreads["d"].s3()
-    spreads["o"].s3()
-
-    pair_at = at
-    at += 8
-    rs_at = at
-    at += 8
-
-    def pair(r):
-        return remote(sib_s.at[r], sib_r.at[r], pair_at + r, sibling)
-
-    def chip(r, m):
-        return remote(rs_s.at[r], rs_r.at[wc], rs_at + r, {"wide": 2 * m + c})
-
-    def column(r):
-        return lax.rem(wc + 1 + r, NWC)
-
-    def terms(m, side):
-        cols = pl.ds(pl.multiple_of(side * feats, feats), feats)
-        return jnp.dot(hid[...], wd[m, :, cols], preferred_element_type=F32) + jnp.dot(
-            attn[...], wo[m, :, cols], preferred_element_type=F32
+    sd.complete()
+    so.complete()
+
+    sum_at = at
+    at += 3
+    part_at = at
+    at += 4
+    span = wd.shape[2]
+
+    def terms(m):
+        return jnp.dot(hid[...], wd[m], preferred_element_type=F32) + jnp.dot(
+            attn[...], wo[m], preferred_element_type=F32
         )
 
-    def forward(r):
-        pair(r).wait_recv()
-        rs_s[r] = (own_s[r].astype(F32) + sib_r[r].astype(F32)).astype(BF16)
-        chip(r, column(r)).start()
-
-    @pl.loop(0, NWC)
-    def _(r):
-        m = column(r)
-        sib_s[r] = terms(m, 1 - c).astype(BF16)
-        pair(r).start()
-        own_s[r] = terms(m, c).astype(BF16)
-
-        @pl.when(r >= 1)
-        def _():
-            forward(r - 1)
-
-    last = NWC - 1
-    pair(last).wait_recv()
-    for r in range(last):
-        src = lax.rem(wc + NWC - 1 - r, NWC)
-        remote(rs_r.at[src], rs_r.at[src], rs_at + r, sibling).wait_recv()
-    rs_r[wc] = jnp.zeros((tokens, feats), BF16)
+    def to_y(r):
+        m = {"wide": (2 * lax.rem(y + 1 + r, 4) + zl) * 2 + c}
+        return remote(ry_s.at[r], ry_r.at[r], sum_at + r, m)
+
+    for r in range(3):
+
+        @pl.loop(0, 2)
+        def _(j):
+            cols = pl.ds(pl.multiple_of(j * span, span), span)
+            ry_s[r, :, cols] = terms(2 * lax.rem(y + 1 + r, 4) + j).astype(BF16)
+
+        to_y(r).start()
+
+    @pl.loop(0, 2)
+    def _(j):
+        cols = pl.ds(pl.multiple_of(j * span, span), span)
+        acc[:, cols] = terms(2 * y + j)
+
+    for r in range(3):
+        to_y(r).wait_recv()
+    spot = 2 * zh + zl
+
+    def to_z(i):
+        m = {"narrow": 2 * x + c, "wide": 4 * y + i}
+        return remote(rz_s.at[i], rz_r.at[spot], part_at + i, m, part_at + spot)
+
+    for i in range(4):
+        cols = slice(i * feats, (i + 1) * feats)
+
+        @pl.loop(0, tokens // 64)
+        def _(k):
+            r = pl.ds(pl.multiple_of(k * 64, 64), 64)
+            total = acc[r, cols]
+            for m in range(3):
+                total = total + ry_r[m, r, cols].astype(F32)
+            rz_s[i, r, :] = total.astype(BF16)
+
+        mine = jnp.logical_and(home, 2 * zl + c == i)
+
+        @pl.when(jnp.logical_not(mine))
+        def _():
+            to_z(i).start()
+
+        @pl.when(mine)
+        def _():
+            rz_r[spot] = rz_s[i]
+
+    for i in range(4):
+
+        @pl.when(jnp.logical_not(jnp.logical_and(home, spot == i)))
+        def _():
+            remote(rz_r.at[i], rz_r.at[i], part_at, sibling, part_at + i).wait_recv()
 
     @pl.loop(0, tokens // 64)
     def _(i):
         r = pl.ds(pl.multiple_of(i * 64, 64), 64)
-        total = own_s[last, r, :].astype(F32) + sib_r[last, r, :].astype(F32)
-        for m in range(NWC):
-            total = total + rs_r[m, r, :].astype(F32)
-        out_ref[r, :] = (xs[w, r, :].astype(F32) + total).astype(BF16)
+        total = rz_r[0, r, :].astype(F32)
+        for m in range(1, 4):
+            total = total + rz_r[m, r, :].astype(F32)
+        out_ref[r, :] = (resid[r, :].astype(F32) + total).astype(BF16)
 
     tail = out_ref[tokens - 16 : tokens, :].astype(F32)
     last_n[n] = jnp.broadcast_to(tail[15:16, :], (8, feats))
@@ -601,13 +671,35 @@
         copy.wait_send()
     for name in names:
         spreads[name].finish()
-    for r in range(NWC):
-        pair(r).wait_send()
-    for r in range(last):
-        chip(r, column(r)).wait_send()
-
-
-def layer(rows, wq, wu, wd, wo, pk, pv, sk, sv, gains, cos_t, sin_a, sin_b, bias):
+    for d, e in ((0, 1), (1, 0), (1, 1)):
+        over_z(d, e).wait_send()
+    for i in range(4):
+        for d in range(1, 4):
+            over_y(i, d).wait_send()
+    for j in range(2):
+        for d in range(4):
+            for e in range(2):
+                if d or e:
+                    over_x(j, d, e).wait_send()
+
+    @pl.when(away)
+    def _():
+        over_z(0, 0).wait_send()
+        for j, (src, dst) in enumerate(suffix):
+            remote(src, dst, suffix_at + j, swap).wait_send()
+        for j in range(2):
+            over_x(j, 0, 0).wait_send()
+
+    for r in range(3):
+        to_y(r).wait_send()
+    for i in range(4):
+
+        @pl.when(jnp.logical_not(jnp.logical_and(home, 2 * zl + c == i)))
+        def _():
+            to_z(i).wait_send()
+
+
+def layer(rows, wq, wu, wd, wo, pk, pv, sk, sv, owner, gains, cos_t, sin_a, sin_b, bias):
     tokens = rows.shape[0] // NN
     feats = rows.shape[1]
     dim = 2 * NWC * feats
@@ -616,15 +708,15 @@
     vm = pltpu.VMEM
     anywhere = pl.BlockSpec(memory_space=pl.ANY)
     inside = pl.BlockSpec(memory_space=pltpu.VMEM)
-    modes = {"q": True, "d": True, "o": True, "u": True}
-    blocks = (NWC, tokens, feats)
+    four = (4, tokens, feats)
+    groups = (3, tokens, 4 * feats)
     return pl.pallas_call(
-        functools.partial(layer_kernel, modes),
+        layer_kernel,
         out_shape=(
             jax.ShapeDtypeStruct((tokens, feats), BF16),
             jax.ShapeDtypeStruct((NN, dim), F32),
         ),
-        in_specs=[anywhere] * 9 + [inside] * 5,
+        in_specs=[anywhere] * 9 + [inside] * 6,
         out_specs=(inside, inside),
         scratch_shapes=[
             vm((NN,) + wq.shape, BF16),
@@ -636,6 +728,7 @@
             vm(sk.shape[1:], BF16),
             vm(sv.shape[1:], BF16),
             vm((NN, tokens, feats), BF16),
+            vm((tokens, feats), BF16),
             vm((2 * NWC, tokens, feats), BF16),
             vm((tokens, dim), BF16),
             vm((tokens, dim), BF16),
@@ -645,11 +738,10 @@
             vm((tokens, feats), BF16),
             vm((tokens, wu.shape[1]), F32),
             vm((tokens, wu.shape[1]), BF16),
-            vm(blocks, BF16),
-            vm(blocks, BF16),
-            vm(blocks, BF16),
-            vm((NWC - 1, tokens, feats), BF16),
-            vm(blocks, BF16),
+            vm(groups, BF16),
+            vm(groups, BF16),
+            vm(four, BF16),
+            vm(four, BF16),
             vm((NN, 8, feats), F32),
             vm((2 * NWC, 8, feats), F32),
             pltpu.SemaphoreType.DMA((112,)),
@@ -659,7 +751,7 @@
         compiler_params=pltpu.CompilerParams(
             collective_id=1, has_side_effects=True, vmem_limit_bytes=VMEM_LIMIT
         ),
-    )(rows, wq, wu, wd, wo, pk, pv, sk, sv, gains, cos_t, sin_a, sin_b, bias)
+    )(rows, wq, wu, wd, wo, pk, pv, sk, sv, owner, gains, cos_t, sin_a, sin_b, bias)
 
 
 def body(
@@ -685,14 +777,13 @@
     all_ids = gather_ids(token_ids)
     vocab_rows = embedding.shape[0]
     local_ids = all_ids - n * vocab_rows
-    inside = (local_ids >= 0) & (local_ids < vocab_rows)
     rows = jnp.take(embedding, jnp.clip(local_ids, 0, vocab_rows - 1), axis=0)
-    rows = jnp.where(inside[:, None], rows, jnp.zeros((), BF16))
+    owner = jnp.broadcast_to((token_ids // vocab_rows)[:, None], (stretch, embedding.shape[1]))
 
     second = (group_ids == 1)[:, None, None]
     pk = jnp.where(second, prefix_keys[1][None], prefix_keys[0][None])
     pv = jnp.where(second, prefix_values[1][None], prefix_values[0][None])
-    me = n[None]
+    me = (2 * (n // 2) + lax.axis_index("wide") % 2)[None]
     group = pick(group_ids, me)
     far = pick(prefix_lengths, group)[0]
     cached = pick(cached_lengths, me)[0]
@@ -725,6 +816,7 @@
         pv,
         suffix_keys,
         suffix_values,
+        owner,
         ln_gains,
         cos_t,
         sin_a,

time: 380 us -> 341 us (0.90)
  Pallas kernels: 334 us -> 296 us
    pallas_call x1, Pallas kernels: 309 us -> 271 us  [layer(): pl.pallas_call(layer_kernel, out_shape=(jax.ShapeDtypeStruct((tokens, fea...]
    select_n x1, other arithmetic: 5.76 us -> 0.7 us  [body(): token_ids // vocab_rows]
where the time goes in v2:
time: 341 us; the launch traced here: 340 us
  Pallas kernels  296 us (87%)
  local copies, waits for them, and re-layouts  22.9 us (7%)
  other arithmetic  16.2 us (5%)
    pallas_call x1, Pallas kernels, layer(): pl.pallas_call(layer_kernel, out_shape=(jax.ShapeDtypeStruct((tokens, fea...  271 us
    gather x1, local copies, waits for them, and re-layouts, body(): rows = jnp.take(embedding, jnp.clip(local_ids, 0, vocab_rows - 1), axis=0)  16.9 us
    pallas_call x1, Pallas kernels, max_over_all(): pl.pallas_call(max_kernel, out_shape=jax.ShapeDtypeStruct((8, 128), F32),...  13.9 us
    pallas_call x1, Pallas kernels, gather_ids(): pl.pallas_call(ids_kernel, out_shape=jax.ShapeDtypeStruct((NN, 4, 128), j...  10.6 us

profile of v2, /device:TPU:1, one launch (start us, length us, event | category | flops | bytes accessed | tf_op | source)
XLA Modules:
  0.0 340.0 jit_solution(12011046269279321076)
XLA Ops:
  0.7 0.8 broadcast_compare_fusion
  1.6 1.3 fusion.5
  3.0 1.9 fusion.7
  6.9 0.7 iota_compare_fusion
  7.5 0.7 add_select_fusion.1
  8.3 10.6 %shard_map.175 = s32[8,4,128]{2,1,0:T(4,128)} custom-call(s32[4,128]{1,0:T(4,128)} %bitcast.16), custom_call_target="tpu_custom_call" | custom-call | tf_op jit(solution)/shard_map/pallas_call | solution.py:72
  18.9 0.7 subtract_clamp_fusion
  20.3 0.8 slice_bitcast_fusion.1
  21.1 0.9 broadcast_select_fusion.1
  22.0 0.9 broadcast_in_dim.127.owner
  22.9 1.0 multiply_sine_fusion
  23.9 0.9 maximum_maximum_fusion.1.sin_b
  24.8 0.9 maximum_maximum_fusion.cos_t
  25.6 0.7 concatenate.17.sin_a
  26.4 16.9 %gather_fusion = bf16[4096,256]{1,0:T(8,128)(2,1)} fusion(bf16[6304,256]{1,0:T(8,128)(2,1)S(1)} %copy-done, s32[4096]{0:T(1024)S(1)} %broadcast_clamp_fusion), kind=kCustom, calls=%fused_computation | custom fusion | bytes 4210688 | tf_op jit(solution)/shard_map/jit(_take)/gather | solution.py:780
  43.3 3.0 broadcast_select_fusion.rows
  46.3 271.3 %shard_map.176 = (bf16[512,256]{1,0:T(8,128)(2,1)}, f32[8,4096]{1,0:T(8,128)}) custom-call(bf16[4096,256]{1,0:T(8,128)(2,1)} %broadcast_select_fusion.rows, bf16[512,768]{1,0:T(8,128)(2,1)} %wq_in.1, bf16[512,1024]{1,0:T(8,128)(2,1)} %wu_in.1, bf16[1024,512]{1,0:T(8,128)(2,1)} %wd_in.1, bf16[256,512]{1,0:T(8,128)(2,1)} %wo_in.1, ...), custom_call_target="tpu_custom_call" | custom-call | tf_op jit(solution)/shard_map/pallas_call | solution.py:713
  317.5 1.1 reduce_sum.58
  318.6 1.1 multiply_reduce_fusion
  319.8 3.1 convolution_reduce_fusion
  323.4 0.7 broadcast_in_dim.137.val_ref
  324.1 13.9 %shard_map.177 = f32[8,128]{1,0:T(8,128)} custom-call(f32[8,128]{1,0:T(8,128)} %broadcast_in_dim.137.val_ref), custom_call_target="tpu_custom_call" | custom-call | tf_op jit(solution)/shard_map/pallas_call | solution.py:127
  338.0 1.3 slice_reduce_fusion
  339.3 0.7 copy.21
  (24 shorter events, 2.1 us)
Async XLA Ops:
  0.6 25.8 %copy-start = (bf16[6304,256]{1,0:T(8,128)(2,1)S(1)}, bf16[6304,256]{1,0:T(8,128)(2,1)}, u32[]{:S(2)}) copy-start(bf16[6304,256]{1,0:T(8,128)(2,1)} %param.20) | copy-start | bytes 9682948
  46.3 273.5 %copy-start.2 = (f32[4096]{0:T(1024)S(1)}, f32[4096]{0:T(1024)}, u32[]{:S(2)}) copy-start(f32[4096]{0:T(1024)} %param.30) | copy-start | bytes 49156
  317.5 21.8 %copy-start.1 = (bf16[512,256]{1,0:T(8,128)(2,1)S(1)}, bf16[512,256]{1,0:T(8,128)(2,1)}, u32[]{:S(2)}) copy-start(bf16[512,256]{1,0:T(8,128)(2,1)} %get-tuple-element.25) | copy-start | bytes 786436

commit v3 on v2

--- a/solution.py
+++ b/solution.py
@@ -160,7 +160,7 @@
         )
 
     def fan(self, src):
-        for i, d in enumerate((2, 6, 4)):
+        for i, d in enumerate((2, 6)):
             self.copy(i, src, self.first, {"narrow": lax.rem(self.n + d, NN)}).start()
         self.copy(3, src, self.first, self.sibling).start()
 
@@ -191,10 +191,29 @@
         def _():
             self.local().wait()
 
+    def half(self, h, m):
+        size = self.buf.shape[1] // 2
+        part = self.buf.at[m, pl.ds(h * size, size)]
+        return pltpu.make_async_remote_copy(
+            src_ref=part,
+            dst_ref=part,
+            send_sem=self.ssem.at[self.base + (2, 8)[h]],
+            recv_sem=self.rsem.at[self.base + (2, 8)[h]],
+            device_id={"narrow": lax.rem(self.n + (2, 6)[h], NN)},
+            device_id_type=MESH,
+        )
+
+    def pass_on(self):
+        for i, m in enumerate(self.arrivals[:2]):
+            self.copy(i, self.buf.at[m], m, self.sibling).wait_recv()
+            self.half(i, m).start()
+            self.copy(4 + i, self.buf.at[m], m, self.sibling).start()
+
     def share(self):
-        for i, m in enumerate(self.arrivals):
-            self.copy(i, self.buf.at[m], m, self.sibling).wait_recv()
-            self.copy(4 + i, self.buf.at[m], m, self.sibling).start()
+        m = self.arrivals[2]
+        for h in range(2):
+            self.half(h, m).wait_recv()
+        self.copy(6, self.buf.at[m], m, self.sibling).start()
 
     def others(self):
         flip = 1 - 2 * self.c
@@ -205,8 +224,10 @@
             self.copy(3 + i, self.buf.at[m], m, self.sibling).wait_recv()
 
     def finish(self):
-        for i in range(7):
+        for i in (0, 1, 3, 4, 5, 6):
             self.copy(i, self.buf.at[self.first], self.first, self.sibling).wait_send()
+        for h in range(2):
+            self.half(h, self.first).wait_send()
 
         @pl.when(self.away)
         def _():
@@ -299,9 +320,9 @@
     names = ["q", "d", "o", "u"]
     spreads = {}
     for k, (name, own, buf) in enumerate(zip(names, (wq_in, wd_in, wo_in, wu_in), (wq, wd, wo, wu))):
-        spreads[name] = Spread(own, buf, 8 * k, (ssem, rsem, lsem.at[k]), place)
+        spreads[name] = Spread(own, buf, 9 * k, (ssem, rsem, lsem.at[k]), place)
     sq, sd, so, su = (spreads[name] for name in names)
-    at = 32
+    at = 36
     sends = []
 
     emb_at = at
@@ -413,13 +434,14 @@
     so.start_away()
     su.start_home()
     su.start_away()
-    sq.share()
+    sq.pass_on()
     sd.relay()
     for i in range(4):
         for d in range(1, 4):
             block = 4 * lax.rem(y + 4 - d, 4) + i
             remote(xs.at[block], xs.at[block], y_at + 4 * (d - 1) + i, sibling).wait_recv()
 
+    sq.share()
     total_feats = wide * feats
 
     @pl.loop(0, tokens // 32)
@@ -442,6 +464,7 @@
 
     so.relay()
     su.relay()
+    sd.pass_on()
     sq.complete()
 
     @pl.loop(0, wq.shape[2] // 256)
@@ -535,9 +558,11 @@
             attn[r, hc] = (num / den).astype(BF16)
 
     attend(0)
+    so.pass_on()
+    su.pass_on()
+    attend(1)
     so.share()
     su.share()
-    attend(1)
 
     def up_rows(m, fresh):
         k = pl.ds(pl.multiple_of(m * wu.shape[1], wu.shape[1]), wu.shape[1])
@@ -777,7 +802,7 @@
     all_ids = gather_ids(token_ids)
     vocab_rows = embedding.shape[0]
     local_ids = all_ids - n * vocab_rows
-    rows = jnp.take(embedding, jnp.clip(local_ids, 0, vocab_rows - 1), axis=0)
+    rows = embedding.at[jnp.clip(local_ids, 0, vocab_rows - 1)].get(mode="promise_in_bounds")
     owner = jnp.broadcast_to((token_ids // vocab_rows)[:, None], (stretch, embedding.shape[1]))
 
     second = (group_ids == 1)[:, None, None]

time: 341 us -> 329 us (0.965)
  Pallas kernels: 296 us -> 287 us
    pallas_call x1, Pallas kernels: 271 us -> 263 us  [layer(): pl.pallas_call(layer_kernel, out_shape=(jax.ShapeDtypeStruct((tokens, fea...]
where the time goes in v3:
time: 329 us
  Pallas kernels  287 us (87%)
  local copies, waits for them, and re-layouts  22.9 us (7%)
  other arithmetic  13.2 us (4%)
    pallas_call x1, Pallas kernels, layer(): pl.pallas_call(layer_kernel, out_shape=(jax.ShapeDtypeStruct((tokens, fea...  263 us
    gather x1, local copies, waits for them, and re-layouts, body(): embedding.at[jnp.clip(local_ids, 0, vocab_rows - 1)]  16.9 us
    pallas_call x1, Pallas kernels, max_over_all(): pl.pallas_call(max_kernel, out_shape=jax.ShapeDtypeStruct((8, 128), F32),...  14.2 us
    pallas_call x1, Pallas kernels, gather_ids(): pl.pallas_call(ids_kernel, out_shape=jax.ShapeDtypeStruct((NN, 4, 128), j...  10.6 us

profile of v3, /device:TPU:1, one launch (start us, length us, event | category | flops | bytes accessed | tf_op | source)
XLA Modules:
  0.0 328.7 jit_solution(5682684452689561661)
XLA Ops:
  0.7 0.8 broadcast_compare_fusion
  1.7 1.3 fusion.5
  3.0 1.9 fusion.7
  6.2 0.7 iota_compare_fusion.1
  6.9 0.7 iota_compare_fusion
  7.5 0.7 add_select_fusion.1
  8.3 10.6 %shard_map.175 = s32[8,4,128]{2,1,0:T(4,128)} custom-call(s32[4,128]{1,0:T(4,128)} %bitcast.14), custom_call_target="tpu_custom_call" | custom-call | tf_op jit(solution)/shard_map/pallas_call | solution.py:72
  18.9 0.7 subtract_clamp_fusion
  20.3 0.8 slice_bitcast_fusion.1
  21.1 0.9 broadcast_select_fusion
  22.0 0.9 broadcast_in_dim.116.owner
  22.9 1.0 multiply_sine_fusion
  23.9 0.8 maximum_maximum_fusion.1.sin_b
  24.8 0.9 maximum_maximum_fusion.cos_t
  25.6 0.7 concatenate.17.sin_a
  26.4 16.9 %gather_fusion = bf16[4096,256]{1,0:T(8,128)(2,1)} fusion(bf16[6304,256]{1,0:T(8,128)(2,1)S(1)} %copy-done, s32[4096]{0:T(1024)S(1)} %broadcast_clamp_fusion), kind=kCustom, calls=%fused_computation | custom fusion | bytes 4210688 | tf_op jit(solution)/shard_map/gather | solution.py:805
  43.3 262.6 %shard_map.176 = (bf16[512,256]{1,0:T(8,128)(2,1)}, f32[8,4096]{1,0:T(8,128)}) custom-call(bf16[4096,256]{1,0:T(8,128)(2,1)} %gather_fusion, bf16[512,768]{1,0:T(8,128)(2,1)} %wq_in.1, bf16[512,1024]{1,0:T(8,128)(2,1)} %wu_in.1, bf16[1024,512]{1,0:T(8,128)(2,1)} %wd_in.1, bf16[256,512]{1,0:T(8,128)(2,1)} %wo_in.1, ...), custom_call_target="tpu_custom_call" | custom-call | tf_op jit(solution)/shard_map/pallas_call | solution.py:738
  305.9 1.1 reduce_sum.58
  307.0 1.1 multiply_reduce_fusion
  308.1 3.1 convolution_reduce_fusion
  311.8 0.7 broadcast_in_dim.126.val_ref
  312.4 14.2 %shard_map.177 = f32[8,128]{1,0:T(8,128)} custom-call(f32[8,128]{1,0:T(8,128)} %broadcast_in_dim.126.val_ref), custom_call_target="tpu_custom_call" | custom-call | tf_op jit(solution)/shard_map/pallas_call | solution.py:127
  326.7 1.3 slice_reduce_fusion
  328.0 0.7 copy.21
  (22 shorter events, 1.4 us)
Async XLA Ops:
  0.6 25.7 %copy-start = (bf16[6304,256]{1,0:T(8,128)(2,1)S(1)}, bf16[6304,256]{1,0:T(8,128)(2,1)}, u32[]{:S(2)}) copy-start(bf16[6304,256]{1,0:T(8,128)(2,1)} %param.20) | copy-start | bytes 9682948
  43.3 264.9 %copy-start.2 = (f32[4096]{0:T(1024)S(1)}, f32[4096]{0:T(1024)}, u32[]{:S(2)}) copy-start(f32[4096]{0:T(1024)} %param.30) | copy-start | bytes 49156
  305.9 22.1 %copy-start.1 = (bf16[512,256]{1,0:T(8,128)(2,1)S(1)}, bf16[512,256]{1,0:T(8,128)(2,1)}, u32[]{:S(2)}) copy-start(bf16[512,256]{1,0:T(8,128)(2,1)} %get-tuple-element.25) | copy-start | bytes 786436

commit v4 on v3

--- a/solution.py
+++ b/solution.py
@@ -557,9 +557,9 @@
             num = num + jnp.dot(probs[:, lo : lo + tokens], qkv[:, v_cols], preferred_element_type=F32)
             attn[r, hc] = (num / den).astype(BF16)
 
-    attend(0)
     so.pass_on()
     su.pass_on()
+    attend(0)
     attend(1)
     so.share()
     su.share()

time: 329 us -> 326 us (level)
  no operation moved by 1% of the time
where the time goes in v4:
time: 326 us
  Pallas kernels  285 us (87%)
  local copies, waits for them, and re-layouts  22.9 us (7%)
  other arithmetic  13.2 us (4%)
    pallas_call x1, Pallas kernels, layer(): pl.pallas_call(layer_kernel, out_shape=(jax.ShapeDtypeStruct((tokens, fea...  260 us
    gather x1, local copies, waits for them, and re-layouts, body(): embedding.at[jnp.clip(local_ids, 0, vocab_rows - 1)]  16.9 us
    pallas_call x1, Pallas kernels, max_over_all(): pl.pallas_call(max_kernel, out_shape=jax.ShapeDtypeStruct((8, 128), F32),...  14.4 us
    pallas_call x1, Pallas kernels, gather_ids(): pl.pallas_call(ids_kernel, out_shape=jax.ShapeDtypeStruct((NN, 4, 128), j...  10.6 us

profile of v4, /device:TPU:1, one launch (start us, length us, event | category | flops | bytes accessed | tf_op | source)
XLA Modules:
  0.0 325.9 jit_solution(5958453821542187702)
XLA Ops:
  0.7 0.8 broadcast_compare_fusion
  1.7 1.3 fusion.5
  3.0 1.9 fusion.7
  6.2 0.7 iota_compare_fusion.1
  6.9 0.7 iota_compare_fusion
  7.5 0.7 add_select_fusion.1
  8.3 10.6 %shard_map.175 = s32[8,4,128]{2,1,0:T(4,128)} custom-call(s32[4,128]{1,0:T(4,128)} %bitcast.14), custom_call_target="tpu_custom_call" | custom-call | tf_op jit(solution)/shard_map/pallas_call | solution.py:72
  18.9 0.7 subtract_clamp_fusion
  20.3 0.8 slice_bitcast_fusion.1
  21.1 0.9 broadcast_select_fusion
  22.0 0.9 broadcast_in_dim.116.owner
  22.9 1.0 multiply_sine_fusion
  23.9 0.8 maximum_maximum_fusion.1.sin_b
  24.8 0.9 maximum_maximum_fusion.cos_t
  25.6 0.7 concatenate.17.sin_a
  26.4 16.9 %gather_fusion = bf16[4096,256]{1,0:T(8,128)(2,1)} fusion(bf16[6304,256]{1,0:T(8,128)(2,1)S(1)} %copy-done, s32[4096]{0:T(1024)S(1)} %broadcast_clamp_fusion), kind=kCustom, calls=%fused_computation | custom fusion | bytes 4210688 | tf_op jit(solution)/shard_map/gather | solution.py:805
  43.3 259.7 %shard_map.176 = (bf16[512,256]{1,0:T(8,128)(2,1)}, f32[8,4096]{1,0:T(8,128)}) custom-call(bf16[4096,256]{1,0:T(8,128)(2,1)} %gather_fusion, bf16[512,768]{1,0:T(8,128)(2,1)} %wq_in.1, bf16[512,1024]{1,0:T(8,128)(2,1)} %wu_in.1, bf16[1024,512]{1,0:T(8,128)(2,1)} %wd_in.1, bf16[256,512]{1,0:T(8,128)(2,1)} %wo_in.1, ...), custom_call_target="tpu_custom_call" | custom-call | tf_op jit(solution)/shard_map/pallas_call | solution.py:738
  303.0 1.1 reduce_sum.58
  304.1 1.1 multiply_reduce_fusion
  305.2 3.1 convolution_reduce_fusion
  308.9 0.7 broadcast_in_dim.126.val_ref
  309.5 14.4 %shard_map.177 = f32[8,128]{1,0:T(8,128)} custom-call(f32[8,128]{1,0:T(8,128)} %broadcast_in_dim.126.val_ref), custom_call_target="tpu_custom_call" | custom-call | tf_op jit(solution)/shard_map/pallas_call | solution.py:127
  323.9 1.3 slice_reduce_fusion
  325.2 0.7 copy.21
  (22 shorter events, 1.4 us)
Async XLA Ops:
  0.6 25.7 %copy-start = (bf16[6304,256]{1,0:T(8,128)(2,1)S(1)}, bf16[6304,256]{1,0:T(8,128)(2,1)}, u32[]{:S(2)}) copy-start(bf16[6304,256]{1,0:T(8,128)(2,1)} %param.20) | copy-start | bytes 9682948
  43.3 261.9 %copy-start.2 = (f32[4096]{0:T(1024)S(1)}, f32[4096]{0:T(1024)}, u32[]{:S(2)}) copy-start(f32[4096]{0:T(1024)} %param.30) | copy-start | bytes 49156
  302.9 22.3 %copy-start.1 = (bf16[512,256]{1,0:T(8,128)(2,1)S(1)}, bf16[512,256]{1,0:T(8,128)(2,1)}, u32[]{:S(2)}) copy-start(bf16[512,256]{1,0:T(8,128)(2,1)} %get-tuple-element.25) | copy-start | bytes 786436
